TPU v7x, 32 devices: a whole 2x2x4 slice. The times are simulated.
32 devices in a mesh: seq: 8 (over z, y), ffn: 4 (over x, core).
Axes of the slice: x: 2, y: 2, z: 4, core: 2. Of those that a mesh axis runs over, the one named last changes fastest.
Arguments:
- child_feat: bfloat16 [4096, 1024], P('seq'), may hold values from -6 to 6
- parent_feat: bfloat16 [512, 1024], P('seq'), may hold values from -6 to 6
- child_parent: int32 [4096], P('seq'), may hold values from 0 to 63
- owner: int32 [4096, 1], P('seq'), may hold values from 0 to 7; in each aligned block of 512 rows (0 to 511, 512 to 1023, ...) at most 128 rows name the same one
- log_gate: float32 [16, 8192], P('ffn', 'seq'), may hold values from -1 to 0
- norm_gain: bfloat16 [1024], replicated, may hold values from 0.3984375 to 1.59375
- w_query: bfloat16 [1024, 1024], P(None, 'ffn'), may hold values from -0.1875 to 0.1875
- w_key: bfloat16 [1024, 1024], P(None, 'ffn'), may hold values from -0.1875 to 0.1875
- w_value: bfloat16 [1024, 1024], P(None, 'ffn'), may hold values from -0.1875 to 0.1875
- head_gain: bfloat16 [1024], P('ffn'), may hold values from 0.25 to 1.75
- w_out: bfloat16 [1024, 1024], P('ffn'), may hold values from -0.1875 to 0.1875
- ffn_gain: bfloat16 [1024], replicated, may hold values from 0.3984375 to 1.59375
- w_up: bfloat16 [1024, 4096], P(None, 'ffn'), may hold values from -0.1875 to 0.1875
- w_down: bfloat16 [4096, 1024], P('ffn'), may hold values from -0.09375 to 0.09375
Outputs:
- child_out: bfloat16 [4096, 1024], P('seq', 'ffn')
Inputs may be any that keep to these rules, and one draw needn't show every extreme that they name: The parent of child i is row (i // 512) * 64 + child_parent[i] of parent_feat. Among the 512 children of one index of seq, at most 128 name the same owner, and in every draw some owner is named exactly 128 times by some block.
All inputs are finite; a program needn't handle non-finite values.
Results may differ from a plain program's by a relative error of at most 0.013.
Values may be sent and summed in bfloat16 or wider, within the bound.
No kernel may reach another device: no remote copies, remote signals or barrier semaphores. Data moves between devices by JAX's collectives and lax.ppermute only.
A program may use at most 64 MiB of HBM per device.

v0:
```python
import jax
import jax.numpy as jnp
from jax import lax
from jax.sharding import PartitionSpec as P

D = 1024
HD = 64
PAR_DEV = 64
SLOT_DEV = 1024


EPSILON = 1e-05
PRECISE = lax.Precision.HIGHEST


def prefix_2(array, axis, combine, identity):
    peers, mine = (lax.axis_size(axis), lax.axis_index(axis))
    everything = jax.tree.map(
        lambda part, kind: lax.all_gather(part.astype(kind), axis),
        array,
        (jnp.bfloat16, jnp.bfloat16),
    )
    start = jax.tree.map(
        lambda part, zero: jnp.broadcast_to(jnp.asarray(zero, part.dtype), part.shape),
        array,
        identity,
    )

    def step(k, before):
        reached = k < mine
        new = combine(
            before, jax.tree.map(lambda part, own: part[k].astype(own.dtype), everything, array)
        )
        return jax.tree.map(lambda a, b: jnp.where(reached, a, b), new, before)

    return lax.fori_loop(0, peers, step, start)


def row_norm(values, scales):
    return values * lax.rsqrt(jnp.mean(values * values, axis=-1, keepdims=True) + EPSILON) * scales


def on_device(
    child_feat,
    parent_feat,
    child_parent,
    owner,
    log_gate,
    norm_gain,
    w_query,
    w_key,
    w_value,
    head_gain,
    w_out,
    ffn_gain,
    w_up,
    w_down,
):
    seq_count = lax.axis_size("seq")
    ffn_count = lax.axis_size("ffn")
    capacity = SLOT_DEV // seq_count
    column_share = D // ffn_count
    ffn_index = lax.axis_index("ffn")
    local_heads = log_gate.shape[0]
    parent_pick = (child_parent[:, None] == jnp.arange(PAR_DEV, dtype=jnp.int32)[None, :]).astype(
        jnp.bfloat16
    )
    joined = (
        child_feat.astype(jnp.float32)
        + jnp.dot(parent_pick, parent_feat, preferred_element_type=jnp.float32)
    ).astype(jnp.bfloat16)
    owner_ids = owner[:, 0]
    matched = (owner_ids[:, None] == jnp.arange(seq_count, dtype=jnp.int32)[None, :]).astype(
        jnp.int32
    )
    within = jnp.sum(matched * (jnp.cumsum(matched, axis=0) - 1), axis=1)
    target = owner_ids * capacity + within
    quarter_cols = lax.dynamic_slice_in_dim(joined, ffn_index * column_share, column_share, 1)
    outgoing = jnp.zeros((SLOT_DEV, column_share), jnp.bfloat16).at[target].set(quarter_cols)
    arrived = lax.all_to_all(
        outgoing.reshape(seq_count, capacity, column_share),
        "seq",
        split_axis=0,
        concat_axis=0,
        tiled=True,
    )
    slot_rows = lax.all_gather(arrived.reshape(SLOT_DEV, column_share), "ffn", axis=1, tiled=True)
    residual_in = slot_rows.astype(jnp.float32)
    normed = row_norm(residual_in, norm_gain.astype(jnp.float32)).astype(jnp.bfloat16)
    queries = (
        jnp.dot(normed, w_query, preferred_element_type=jnp.float32)
        .astype(jnp.bfloat16)
        .reshape(SLOT_DEV, local_heads, HD)
    )
    key_rows = (
        jnp.dot(normed, w_key, preferred_element_type=jnp.float32)
        .astype(jnp.bfloat16)
        .reshape(SLOT_DEV, local_heads, HD)
    )
    value_rows = (
        jnp.dot(normed, w_value, preferred_element_type=jnp.float32)
        .astype(jnp.bfloat16)
        .reshape(SLOT_DEV, local_heads, HD)
    )
    running = jnp.cumsum(log_gate, axis=1)
    position = jnp.arange(SLOT_DEV, dtype=jnp.int32)
    causal = (position[:, None] >= position[None, :])[None]
    spacing = running[:, :, None] - running[:, None, :]
    decay_mat = jnp.where(causal, jnp.exp(jnp.where(causal, spacing, 0.0)), 0.0)
    scores = jnp.einsum("shd,thd->hst", queries, key_rows, preferred_element_type=jnp.float32)
    mixing = (scores * decay_mat).astype(jnp.bfloat16)
    inside = jnp.einsum("hst,thd->shd", mixing, value_rows, preferred_element_type=jnp.float32)
    block_end = running[:, -1]
    fading = jnp.exp(block_end[:, None] - running).T
    local_state = jnp.einsum(
        "shd,she->hde",
        key_rows.astype(jnp.float32) * fading[:, :, None],
        value_rows.astype(jnp.float32),
        precision=PRECISE,
    )
    empty_state = jnp.zeros((local_heads, HD, HD), jnp.float32)

    def compose(earlier, latter):
        return (earlier[0] * latter[0], latter[0][:, None, None] * earlier[1] + latter[1])

    prefix = prefix_2(
        (jnp.exp(block_end), local_state),
        "seq",
        compose,
        (jnp.ones((local_heads,), jnp.float32), empty_state),
    )
    incoming = prefix[1]
    outside = jnp.exp(running).T[:, :, None] * jnp.einsum(
        "shd,hde->she", queries.astype(jnp.float32), incoming, precision=PRECISE
    )
    combined = inside + outside
    head_scales = head_gain.astype(jnp.float32).reshape(local_heads, HD)
    per_head = (
        combined
        * lax.rsqrt(jnp.mean(combined * combined, axis=-1, keepdims=True) + EPSILON)
        * head_scales[None]
    )
    flattened = per_head.astype(jnp.bfloat16).reshape(SLOT_DEV, local_heads * HD)
    projected = jnp.dot(flattened, w_out, preferred_element_type=jnp.float32)
    hidden = residual_in + lax.psum(projected.astype(jnp.bfloat16), "ffn").astype(jnp.float32)
    second = row_norm(hidden, ffn_gain.astype(jnp.float32)).astype(jnp.bfloat16)
    kept_cols = lax.dynamic_slice_in_dim(hidden, ffn_index * column_share, column_share, 1)
    expanded = jax.nn.gelu(jnp.dot(second, w_up, preferred_element_type=jnp.float32)).astype(
        jnp.bfloat16
    )
    ffn_part = lax.psum_scatter(
        jnp.dot(expanded, w_down, preferred_element_type=jnp.float32).astype(jnp.bfloat16),
        "ffn",
        scatter_dimension=1,
        tiled=True,
    ).astype(jnp.float32)
    refined = (kept_cols + ffn_part).astype(jnp.bfloat16)
    returned = lax.all_to_all(
        refined.reshape(seq_count, capacity, column_share),
        "seq",
        split_axis=0,
        concat_axis=0,
        tiled=True,
    )
    return returned.reshape(SLOT_DEV, column_share)[target]


def solution(mesh):
    in_specs = (
        P("seq", None),
        P("seq", None),
        P("seq"),
        P("seq", None),
        P("ffn", "seq"),
        P(),
        P(None, "ffn"),
        P(None, "ffn"),
        P(None, "ffn"),
        P("ffn"),
        P("ffn", None),
        P(),
        P(None, "ffn"),
        P("ffn", None),
    )
    out_specs = P("seq", "ffn")
    return jax.shard_map(
        on_device, mesh=mesh, in_specs=in_specs, out_specs=out_specs, check_vma=False
    )
```

profile of v0, /device:TPU:0, one launch (start us, length us, event | category | flops | bytes accessed | tf_op | source)
XLA Modules:
  0.0 245.2 jit_solution(11922618407329347484)
XLA Ops:
  6.6 0.8 fusion.39
  7.4 1.1 reduce-window.14
  8.6 0.2 slice_reduce_fusion.1
  8.8 0.8 fusion.38
  9.6 0.7 compare_select_fusion
  10.3 2.7 %fusion.36 = f32[512,1024]{1,0:T(8,128)} fusion(bf16[64,1024]{1,0:T(8,128)(2,1)} %param.17, s32[512]{0:T(512)} %param.18), kind=kOutput, calls=%fused_computation.55 | convolution fusion | flops 67141632 | bytes 2230272 | tf_op jit(solution)/shard_map/dot_general | solution.py:70
  13.0 3.0 %scatter_custom_fusion = bf16[1024,256]{1,0:T(8,128)(2,1)S(1)} fusion(s32[512]{0:T(512)S(1)} %bitcast.86, f32[512,1024]{1,0:T(8,128)} %fusion.36, s32[]{:T(128)} %constant.59.clone.1, s32[]{:T(128)S(6)} %select_n.39, bf16[512,1024]{1,0:T(8,128)(2,1)} %param.16, bf16[]{:T(256)} %constant.57.clone.1), kind=kCustom, calls=%fused_computation.51 | custom fusion | flops 393216 | bytes 1311748 | tf_op jit(solution)/shard_map/scatter | solution.py:79
  16.1 21.7 %all_to_all.10 = bf16[8,128,256]{2,1,0:T(8,128)(2,1)} all-to-all(bf16[8,128,256]{2,1,0:T(8,128)(2,1)S(1)} %bitcast.75), channel_id=1, replica_groups=mesh['seq'=8,'ffn'=4] {'seq'}, dimensions={0} | all-to-all | bytes 1048576 | tf_op jit(solution)/shard_map/all_to_all | solution.py:80
  37.9 1.1 reduce-window.16
  39.1 0.2 slice_reduce_fusion
  39.2 0.2 reduce-window.19
  39.4 0.1 add_bitcast_fusion
  39.6 0.1 copy.22
  39.7 0.6 dynamic-slice
  40.9 0.2 dynamic-update-slice
  41.2 19.5 %all-reduce = bf16[32]{0:T(256)(128)(2,1)S(1)} all-reduce(bf16[32]{0:T(256)(128)(2,1)S(1)} %dynamic-update-slice), channel_id=2, replica_groups=mesh['seq'=8,'ffn'=4] {'seq'}, use_global_device_ids=true, to_apply=%add | all-reduce | flops 32 | bytes 128
  60.7 0.1 reshape.175
  60.8 0.1 reshape.158
  60.8 1.3 iota_compare_fusion
  62.1 0.1 exponential_bitcast_fusion.1
  62.3 2.2 fusion.1
  64.5 2.6 %convolution_convert_fusion.1 = bf16[1024,256]{0,1:T(8,128)(2,1)S(1)} fusion(bf16[1024,256]{1,0:T(8,128)(2,1)} %param.23, bf16[1024,1024]{1,0:T(8,128)(2,1)} %all-gather.4.cloned.1.call-done, f32[1024]{0:T(1024)S(1)} %convert_element_type.110, f32[1024]{0:T(1024)S(1)} %add_rsqrt_fusion.2), kind=kOutput, calls=%fused_computation.39 | convolution fusion | flops 541327360 | bytes 3153920 | tf_op jit(solution)/shard_map/dot_general | solution.py:96
  67.1 2.2 convolution_convert_fusion.3
  69.3 0.7 convolution_convert_fusion.4
  70.0 31.5 %all-gather.1 = bf16[32,64,64]{2,1,0:T(8,128)(2,1)S(1)} all-gather(bf16[4,64,64]{2,1,0:T(8,128)(2,1)S(1)} %convolution_convert_fusion.4), channel_id=3, replica_groups=mesh['seq'=8,'ffn'=4] {'seq'}, dimensions={0}, use_global_device_ids=true | all-gather | bytes 294912 | tf_op jit(solution)/shard_map/all_gather | solution.py:19
  101.6 1.0 while.14
  101.6 0.1 fusion.63
  101.7 0.1 fusion.63
  101.8 0.1 fusion.63
  102.0 0.1 fusion.63
  102.1 0.1 fusion.63
  102.2 0.1 fusion.63
  102.3 0.1 fusion.63
  102.5 0.1 fusion.63
  102.6 3.5 %convolution_convert_fusion.2 = bf16[1024,256]{0,1:T(8,128)(2,1)} fusion(bf16[1024,256]{1,0:T(8,128)(2,1)} %param.22, bf16[1024,1024]{1,0:T(8,128)(2,1)} %all-gather.4.cloned.1.call-done, f32[1024]{0:T(1024)S(1)} %convert_element_type.110, f32[1024]{0:T(1024)S(1)} %add_rsqrt_fusion.2), kind=kOutput, calls=%fused_computation.40 | convolution fusion | flops 541327360 | bytes 3153920 | tf_op jit(solution)/shard_map/dot_general | solution.py:91
  106.1 9.2 %fusion.25 = f32[1024,4,64]{0,2,1:T(8,128)} fusion(bf16[1024,4,64]{0,2,1:T(8,128)(2,1)} %bitcast.94, bf16[1024,4,64]{0,2,1:T(8,128)(2,1)} %bitcast.78, bf16[1024,4,64]{0,2,1:T(8,128)(2,1)} %bitcast.92, f32[4,1024]{1,0:T(4,128)S(1)} %bitcast.82, pred[1024,1024]{1,0:T(8,128)(4,1)S(1)} %copy-done.2), kind=kOutput, calls=%fused_computation.35 | convolution fusion | flops 1094713344 | bytes 3686400 | tf_op jit(solution)/shard_map/hst,thd->shd/dot_general | solution.py:112
  115.3 2.2 multiply_reduce_fusion.1
  117.5 0.1 multiply_convert_fusion.7
  117.7 2.1 convolution_convert_fusion
  119.8 0.3 reduce-scatter.2.cloned.1.call-start
  120.1 48.8 %all-reduce.3.cloned.1.call-done = bf16[1024,1024]{1,0:T(8,128)(2,1)} async-done(((bf16[1024,1024]{1,0:T(8,128)(2,1)}), bf16[1024,1024]{1,0:T(8,128)(2,1)}) %all-reduce.3.cloned.1.call-update) | async-done | bytes 2097168 | tf_op jit(solution)/shard_map/psum | solution.py:145
  168.9 4.8 %convert_add_fusion.1 = (f32[1024,1024]{1,0:T(8,128)}, f32[1024]{0:T(1024)S(1)}) fusion(bf16[1024,1024]{1,0:T(8,128)(2,1)} %all-gather.4.cloned.1.call-done, bf16[1024,1024]{1,0:T(8,128)(2,1)} %all-reduce.3.cloned.1.call-done), kind=kLoop, calls=%fused_computation.7 | loop fusion | flops 5241856 | bytes 8392704 | tf_op jit(solution)/shard_map/add | solution.py:145
  173.7 8.9 %fusion.22 = bf16[1024,1024]{1,0:T(8,128)(2,1)} fusion(bf16[1024,1024]{1,0:T(8,128)(2,1)S(1)} %copy-done, bf16[1024,1024]{1,0:T(8,128)(2,1)} %param.28, f32[1024]{0:T(1024)S(1)} %convert_element_type.123, f32[1024]{0:T(1024)S(1)} %add_rsqrt_fusion.1, bf16[1024,1024]{1,0:T(8,128)(2,1)} %all-gather.4.cloned.1.call-done, ...), kind=kOutput, calls=%fused_computation.33 | convolution fusion | flops 4311744512 | bytes 10493952 | tf_op jit(solution)/shard_map/dot_general | solution.py:152
  182.6 31.4 %reduce-scatter.2.cloned.1.call-done = bf16[1024,256]{1,0:T(8,128)(2,1)} async-done(((bf16[1024,1024]{1,0:T(8,128)(2,1)}), bf16[1024,256]{1,0:T(8,128)(2,1)}) %reduce-scatter.2.cloned.1.call-update) | async-done | bytes 524304 | tf_op jit(solution)/shard_map/reduce_scatter | solution.py:151
  214.0 2.3 add_convert_fusion
  216.3 5.5 %all-to-all-start.1 = ((bf16[8,128,256]{2,1,0:T(8,128)(2,1)}), bf16[8,128,256]{2,1,0:T(8,128)(2,1)S(1)}, u32[]{:S(2)}, u32[]{:S(2)}) async-start(bf16[8,128,256]{2,1,0:T(8,128)(2,1)} %bitcast.20), calls=%async_computation.2 | async-start | bytes 1048576 | tf_op jit(solution)/shard_map/all_to_all | solution.py:158
  221.8 14.3 %all-to-all-done.1 = bf16[8,128,256]{2,1,0:T(8,128)(2,1)S(1)} async-done(((bf16[8,128,256]{2,1,0:T(8,128)(2,1)}), bf16[8,128,256]{2,1,0:T(8,128)(2,1)S(1)}, u32[]{:S(2)}, u32[]{:S(2)}) %all-to-all-start.1) | async-done | bytes 524320 | tf_op jit(solution)/shard_map/all_to_all | solution.py:158
  236.1 2.6 %gather_fusion = bf16[512,256]{1,0:T(8,128)(2,1)} fusion(bf16[1024,256]{1,0:T(8,128)(2,1)S(1)} %bitcast.73, s32[1024]{0:T(1024)S(1)} %pad_clamp_fusion), kind=kCustom, calls=%fused_computation | custom fusion | bytes 526336 | tf_op jit(solution)/shard_map/gather | solution.py:165
  (50 shorter events, 0.4 us)
Async XLA Ops:
  6.5 167.2 %copy-start = (bf16[1024,1024]{1,0:T(8,128)(2,1)S(1)}, bf16[1024,1024]{1,0:T(8,128)(2,1)}, u32[]{:S(2)}) copy-start(bf16[1024,1024]{1,0:T(8,128)(2,1)} %param.29) | copy-start | bytes 6291460
  6.5 33.1 %copy-start.10 = (u32[32]{0:T(128)S(1)}, u32[32]{0:T(128)}, u32[]{:S(2)}) copy-start(u32[32]{0:T(128)} %constant.76) | copy-start | bytes 388
  6.5 31.4 %copy-start.4 = (f32[4,1024]{1,0:T(4,128)S(1)}, f32[4,1024]{1,0:T(4,128)}, u32[]{:S(2)}) copy-start(f32[4,1024]{1,0:T(4,128)} %param.20) | copy-start | bytes 49156
  6.5 54.1 %copy-start.5 = (bf16[1024]{0:T(1024)(128)(2,1)S(1)}, bf16[1024]{0:T(1024)(128)(2,1)}, u32[]{:S(2)}) copy-start(bf16[1024]{0:T(1024)(128)(2,1)} %param.21) | copy-start | bytes 6148
  6.5 54.2 %copy-start.7 = (bf16[256]{0:T(256)(128)(2,1)S(1)}, bf16[256]{0:T(256)(128)(2,1)}, u32[]{:S(2)}) copy-start(bf16[256]{0:T(256)(128)(2,1)} %param.25) | copy-start | bytes 1540
  6.5 55.7 %all-gather.4.cloned.1.call-start = ((), (), s32[]{:S(2)}) async-start(), calls=%async_computation.3 | async-start | bytes 2621440 | tf_op jit(solution)/shard_map/all_gather | solution.py:87
  37.9 131.0 %all-reduce.3.cloned.1.call-start = ((), (), s32[]{:S(2)}) async-start(), calls=%async_computation.4 | async-start | bytes 4194304 | tf_op jit(solution)/shard_map/psum | solution.py:145
  62.2 4.8 %copy-start.1 = (bf16[1024,1024]{1,0:T(8,128)(2,1)S(1)}, bf16[1024,1024]{1,0:T(8,128)(2,1)}, u32[]{:S(2)}) copy-start(bf16[1024,1024]{1,0:T(8,128)(2,1)} %all-gather.4.cloned.1.call-done) | copy-start | bytes 6291460
  67.1 2.2 copy-start.8
  69.3 32.2 %copy-start.9 = (bf16[1024,256]{0,1:T(8,128)(2,1)}, bf16[1024,256]{0,1:T(8,128)(2,1)S(1)}, u32[]{:S(2)}) copy-start(bf16[1024,256]{0,1:T(8,128)(2,1)S(1)} %convolution_convert_fusion.3) | copy-start | bytes 1572868
  102.6 3.5 %copy-start.2 = (pred[1024,1024]{1,0:T(8,128)(4,1)S(1)}, pred[1024,1024]{1,0:T(8,128)(4,1)}, u32[]{:S(2)}) copy-start(pred[1024,1024]{1,0:T(8,128)(4,1)} %iota_compare_fusion) | copy-start | bytes 3145732
  115.3 2.4 copy-start.3
  115.3 4.8 %copy-start.6 = (bf16[1024]{0:T(1024)(128)(2,1)S(1)}, bf16[1024]{0:T(1024)(128)(2,1)}, u32[]{:S(2)}) copy-start(bf16[1024]{0:T(1024)(128)(2,1)} %param.27) | copy-start | bytes 6148
  119.8 94.2 %reduce-scatter.2.cloned.1.call-start = ((), (), s32[]{:S(2)}) async-start(), calls=%async_computation.5 | async-start | bytes 2621440 | tf_op jit(solution)/shard_map/reduce_scatter | solution.py:151
  216.3 19.8 %all-to-all-start.1 = ((bf16[8,128,256]{2,1,0:T(8,128)(2,1)}), bf16[8,128,256]{2,1,0:T(8,128)(2,1)S(1)}, u32[]{:S(2)}, u32[]{:S(2)}) async-start(bf16[8,128,256]{2,1,0:T(8,128)(2,1)} %bitcast.20), calls=%async_computation.2 | async-start | bytes 1048576 | tf_op jit(solution)/shard_map/all_to_all | solution.py:158
Sparse Core Ops, SparseCore 0:
  38.0 21.8 all-gather.3
  119.9 48.9 all-reduce.2
  182.7 31.2 reduce-scatter.1
where the time goes:
time: 246 us; the launch traced here: 245 us
  waiting for transfers between devices  94.6 us (38%)
  blocking collectives  72.7 us (30%)
  matrix products  34.1 us (14%)
  other arithmetic  19.6 us (8%)
  between operations  14 us (6%)
  starting transfers between devices  5.86 us (2%)
  local copies, waits for them, and re-layouts  4.18 us (2%)
    psum x1, waiting for transfers between devices, on_device(): lax.psum(projected.astype(jnp.bfloat16), 'ffn').astype(jnp.float32)  48.8 us
    all_gather x1, blocking collectives, prefix_2(): lax.all_gather(part.astype(kind), axis)  31.5 us
    reduce_scatter x1, waiting for transfers between devices, on_device(): lax.psum_scatter(jnp.dot(expanded, w_down, preferred_element_type=jnp.flo...  31.4 us
    all_to_all x1, blocking collectives, on_device(): lax.all_to_all(outgoing.reshape(seq_count, capacity, column_share), 'seq'...  21.7 us
    unnamed x1, blocking collectives  19.5 us
    all_to_all x1, waiting for transfers between devices, on_device(): lax.all_to_all(refined.reshape(seq_count, capacity, column_share), 'seq',...  14.3 us
    dot_general x1, matrix products, on_device(): jnp.einsum('hst,thd->shd', mixing, value_rows, preferred_element_type=jnp...  9.22 us
    dot_general x1, matrix products, on_device(): jnp.dot(expanded, w_down, preferred_element_type=jnp.float32)  8.86 us
  transfers between devices with their start and end apart: 4, of which 3 were waited for; matrix products, arithmetic and copies ran while one was open for 2% of the time, Pallas kernels for 0%

commit v1 on v0

v1 whole, which is shorter than its diff:
```python
import functools

import jax
import jax.numpy as jnp
from jax import lax
from jax.experimental import pallas as pl
from jax.experimental.pallas import tpu as pltpu
from jax.sharding import PartitionSpec as P

EPSILON = 1e-05
F32 = jnp.float32
BF16 = jnp.bfloat16
LANES = 128
NT = (((1,), (1,)), ((), ()))
TN = (((0,), (0,)), ((), ()))
VMEM = pl.BlockSpec(memory_space=pltpu.VMEM)


def split3(values):
    high = values.astype(BF16)
    rest = values - high.astype(F32)
    middle = rest.astype(BF16)
    low = (rest - middle.astype(F32)).astype(BF16)
    return high, middle, low


def dot(a, b):
    return jnp.dot(a, b, preferred_element_type=F32)


def iota(shape, dim):
    return lax.broadcasted_iota(jnp.int32, shape, dim)


def row_norm(values, scales):
    return values * lax.rsqrt(jnp.mean(values * values, axis=-1, keepdims=True) + EPSILON) * scales


def column(row, width=LANES):
    return jnp.broadcast_to(row, (width, row.shape[1])).T


def head_of_lane(shape, hd):
    return iota(shape, len(shape) - 1) // hd


def pre_kernel(cap, blocks, cf, pf, pick, own, gain, wq, wk, wv, joined, q, k, v, taken):
    tokens = cf.shape[0]
    parents = pf.shape[0]
    tile = min(256, tokens)
    owners = own[...]
    lane = iota((1, blocks * cap), 1)
    lane_owner, lane_rank = lane // cap, lane % cap
    ones = jnp.ones((tokens, LANES), BF16)
    for at in range(0, tokens, tile):
        rows = pl.ds(at, tile)
        chosen = jnp.where(iota((parents, tile), 0) == pick[:, rows], 1.0, 0.0).astype(BF16)
        added = lax.dot_general(chosen, pf[...], TN, preferred_element_type=F32)
        summed = (cf[rows, :].astype(F32) + added).astype(BF16)
        joined[rows, :] = summed
        normed = row_norm(summed.astype(F32), gain[...].astype(F32)).astype(BF16)
        q[rows, :] = dot(normed, wq[...]).astype(BF16)
        k[rows, :] = dot(normed, wk[...]).astype(BF16)
        v[rows, :] = dot(normed, wv[...]).astype(BF16)
        mine = column(own[:, rows])
        same = (mine[:, :1] == owners) & (iota((tile, tokens), 0) + at >= iota((tile, tokens), 1))
        count = dot(jnp.where(same, 1.0, 0.0).astype(BF16), ones)
        rank = count[:, :1].astype(jnp.int32) - 1
        match = mine[:, :1] == lane_owner
        kept = match & (lane_rank <= rank)
        left = match & (lane_rank > rank)
        taken[rows, :] = jnp.where(kept, 1.0, 0.0).astype(BF16)
        taken[pl.ds(tokens + at, tile), :] = jnp.where(left, 1.0, 0.0).astype(BF16)


def gate_rows(gates, cap, blocks):
    if len(gates.shape) == 3:
        rows = jnp.concatenate([gates[o][:, :cap] for o in range(blocks)], axis=1)
    else:
        rows = gates[...]
    heads = rows.shape[0]
    rows = jnp.concatenate([rows, jnp.zeros((8 - heads, rows.shape[1]), F32)], axis=0)
    return jnp.concatenate([part.astype(F32) for part in split3(rows)], axis=0).astype(BF16)


def state_kernel(cap, blocks, hd, taken, gates, k, v, own, states, c_lanes):
    tokens, share = k.shape
    table = gate_rows(gates, cap, blocks)
    summed = lax.dot_general(taken[...], table, NT, preferred_element_type=F32)
    spread = jnp.where(
        iota((24, share), 0) % 8 == head_of_lane((24, share), hd), 1.0, 0.0
    ).astype(BF16)
    wide = sum(dot(part, spread) for part in split3(summed))
    c_lanes[...] = wide[:tokens]
    faded = k[...].astype(F32) * jnp.exp(wide[tokens:])
    turned = faded.astype(BF16).T
    owners = own[...]
    values = v[...]
    lane_head = head_of_lane((hd, share), hd)

    def one(o, nothing):
        masked = jnp.where(owners == o, turned, jnp.zeros_like(turned))
        full = dot(masked, values)
        packed = jnp.zeros((hd, share), F32)
        for h in range(share // hd):
            packed = jnp.where(lane_head == h, full[h * hd : (h + 1) * hd], packed)
        states[o] = packed.astype(BF16)
        return nothing

    lax.fori_loop(0, blocks, one, 0, unroll=blocks <= 8)


def combine_kernel(blocks, hd, states, decay, back):
    def step(b, carry):
        back[b, :hd, :] = carry.astype(BF16)
        return decay[pl.ds(b, 1), :] * carry + states[b].astype(F32)

    total = lax.fori_loop(
        0, blocks, step, jnp.zeros(states.shape[1:], F32), unroll=blocks <= 8
    ).astype(BF16)
    for b in range(blocks):
        back[b, hd:, :] = total


def inside_kernel(cap, blocks, hd, q, k, v, taken, gates, c_lanes, own, inside):
    tokens, share = q.shape
    heads = share // hd
    table = gate_rows(gates, cap, blocks)
    turned = lax.dot_general(table, taken[:tokens, :], NT, preferred_element_type=F32)
    c_rows = turned[:8] + turned[8:16] + turned[16:]
    tile = min(256, tokens)
    for at in range(0, tokens, tile):
        rows = pl.ds(at, tile)
        reach = at + tile
        mine = column(own[:, rows])[:, :1]
        same = (mine == own[:, :reach]) & (
            iota((tile, reach), 0) + at >= iota((tile, reach), 1)
        )
        queries = q[rows, :]
        keys = k[:reach, :]
        values = v[:reach, :]
        total = jnp.zeros((tile, share), F32)
        for h in range(heads):
            only = head_of_lane((tile, share), hd) == h
            scores = lax.dot_general(
                jnp.where(only, queries, jnp.zeros_like(queries)),
                keys,
                NT,
                preferred_element_type=F32,
            )
            gap = c_lanes[rows, h * hd : h * hd + 1] - c_rows[h : h + 1, :reach]
            decay = jnp.where(same, jnp.exp(jnp.where(same, gap, 0.0)), 0.0)
            mixing = (scores * decay).astype(BF16)
            only = head_of_lane((reach, share), hd) == h
            total += dot(mixing, jnp.where(only, values, jnp.zeros_like(values)))
        inside[rows, :] = total


def outside_kernel(blocks, hd, back, lead, whole, q, own, c_lanes, inside, gain, flat, wide, table):
    tokens, share = q.shape
    heads = share // hd
    mine = column(own[...])[:, :1]
    queries = q[...]
    block_diagonal = iota((share, share), 0) // hd == iota((share, share), 1) // hd

    def step(o, carry):
        state = back[o, :hd, :].astype(F32) + lead[pl.ds(o, 1), :] * carry
        stacked = jnp.concatenate([state] * heads, axis=0)
        at = pl.ds(pl.multiple_of(o * share, share), share)
        table[at, :] = jnp.where(block_diagonal, stacked, 0.0).astype(BF16)
        wide[:, at] = jnp.where(mine == o, queries, jnp.zeros_like(queries))
        return whole[pl.ds(o, 1), :] * carry + back[o, hd:, :].astype(F32)

    lax.fori_loop(0, blocks, step, jnp.zeros((hd, share), F32), unroll=blocks <= 8)
    outside = dot(wide[...], table[...]) * jnp.exp(c_lanes[...])
    combined = inside[...] + outside
    square = combined * combined
    mean = jnp.where(block_diagonal, 1.0 / hd, 0.0).astype(BF16)
    spread = sum(dot(part, mean) for part in split3(square))
    flat[...] = (combined * lax.rsqrt(spread + EPSILON) * gain[...].astype(F32)).astype(BF16)


def ffn_kernel(groups, index, *refs):
    flats, wouts = refs[:groups], refs[groups : 2 * groups]
    joined, gain, w_up, w_down, own, even, odd, scratch = refs[2 * groups :]
    mine = index[0]
    tokens, width = joined.shape
    cols = width // groups
    tile = min(256, tokens)
    for at in range(0, tokens, tile):
        rows = pl.ds(at, tile)
        hidden = joined[rows, :].astype(F32)
        for flat, wout in zip(flats, wouts):
            hidden = hidden + dot(flat[rows, :], wout[...])
        scratch[...] = hidden
        second = row_norm(hidden, gain[...].astype(F32)).astype(BF16)
        expanded = jax.nn.gelu(dot(second, w_up[...])).astype(BF16)
        for j in range(groups):
            target = pl.ds(pl.multiple_of((mine ^ j) * cols, cols), cols)
            piece = dot(expanded, w_down[:, target])
            half = pl.ds((j // 2) * cols, cols)
            if j == 0:
                own[rows, :] = piece + scratch[:, target]
            elif j % 2:
                odd[rows, half] = piece.astype(BF16)
            else:
                even[rows, pl.ds((j // 2 - 1) * cols, cols)] = piece


def flip(array, axis, bit):
    size = lax.axis_size(axis)
    return lax.ppermute(array, axis, [(i, i ^ bit) for i in range(size)])


def gather_flips(array, axis):
    size = lax.axis_size(axis)
    parts = {0: array}
    bit = size // 2
    while bit:
        for k in list(parts):
            parts[k ^ bit] = flip(parts[k], axis, bit)
        bit //= 2
    return [parts[k] for k in range(size)]


def shaped(shape, dtype):
    return jax.ShapeDtypeStruct(shape, dtype)


def exchange(array):
    return lax.all_to_all(array, "seq", split_axis=0, concat_axis=0, tiled=True)


def on_device(
    child_feat,
    parent_feat,
    child_parent,
    owner,
    log_gate,
    norm_gain,
    w_query,
    w_key,
    w_value,
    head_gain,
    w_out,
    ffn_gain,
    w_up,
    w_down,
):
    blocks = lax.axis_size("seq")
    groups = lax.axis_size("ffn")
    mine = lax.axis_index("ffn")
    block = lax.axis_index("seq")
    heads, slots = log_gate.shape
    cap = slots // blocks
    tokens, width = child_feat.shape
    share = w_query.shape[1]
    hd = share // heads
    cols = width // groups

    gates = log_gate.reshape(heads, blocks, cap)
    sums = jnp.sum(gates, axis=2)
    payload = jnp.concatenate(
        [gates.transpose(1, 0, 2), jnp.broadcast_to(sums[None], (blocks, heads, blocks))], axis=2
    )
    arrived = exchange(payload)
    all_sums = arrived[:, :, cap:]
    if cap % LANES:
        arrived = arrived[:, :, :cap].transpose(1, 0, 2).reshape(heads, slots)
    wout_parts = gather_flips(w_out, "ffn")

    own = owner.reshape(1, tokens)
    joined, q, k, v, taken = pl.pallas_call(
        functools.partial(pre_kernel, cap, blocks),
        out_shape=(
            shaped((tokens, width), BF16),
            shaped((tokens, share), BF16),
            shaped((tokens, share), BF16),
            shaped((tokens, share), BF16),
            shaped((2 * tokens, slots), BF16),
        ),
        in_specs=[VMEM] * 8,
        out_specs=[VMEM] * 5,
        name="pre",
    )(
        child_feat,
        parent_feat,
        child_parent.reshape(1, tokens),
        own,
        norm_gain.reshape(1, width),
        w_query,
        w_key,
        w_value,
    )

    states, c_lanes = pl.pallas_call(
        functools.partial(state_kernel, cap, blocks, hd),
        out_shape=(shaped((blocks, hd, share), BF16), shaped((tokens, share), F32)),
        in_specs=[VMEM] * 5,
        out_specs=[VMEM] * 2,
        name="state",
    )(taken, arrived, k, v, own)
    states = exchange(states)

    inside = pl.pallas_call(
        functools.partial(inside_kernel, cap, blocks, hd),
        out_shape=shaped((tokens, share), F32),
        in_specs=[VMEM] * 7,
        out_specs=VMEM,
        name="inside",
    )(q, k, v, taken, arrived, c_lanes, own)

    decay = jnp.repeat(jnp.exp(sums).T, hd, axis=1)
    back = pl.pallas_call(
        functools.partial(combine_kernel, blocks, hd),
        out_shape=shaped((blocks, 2 * hd, share), BF16),
        in_specs=[VMEM] * 2,
        out_specs=VMEM,
        name="combine",
    )(states, decay)
    back = exchange(back)

    before = jnp.arange(blocks, dtype=jnp.int32) < block
    lead = jnp.repeat(jnp.exp(jnp.sum(jnp.where(before, all_sums, 0.0), axis=2)), hd, axis=1)
    whole = jnp.repeat(jnp.exp(jnp.sum(all_sums, axis=2)), hd, axis=1)
    flat = pl.pallas_call(
        functools.partial(outside_kernel, blocks, hd),
        out_shape=shaped((tokens, share), BF16),
        in_specs=[VMEM] * 8,
        out_specs=VMEM,
        scratch_shapes=[
            pltpu.VMEM((tokens, blocks * share), BF16),
            pltpu.VMEM((blocks * share, share), BF16),
        ],
        name="outside",
    )(back, lead, whole, q, own, c_lanes, inside, head_gain.reshape(1, share))

    flat_parts = gather_flips(flat, "ffn")
    half = groups // 2
    kept, even, odd = pl.pallas_call(
        functools.partial(ffn_kernel, groups),
        out_shape=(
            shaped((tokens, cols), F32),
            shaped((tokens, max(half - 1, 1) * cols), F32),
            shaped((tokens, half * cols), BF16),
        ),
        in_specs=[pl.BlockSpec(memory_space=pltpu.SMEM)] + [VMEM] * (2 * groups + 4),
        out_specs=[VMEM] * 3,
        scratch_shapes=[pltpu.VMEM((min(256, tokens), width), F32)],
        name="ffn",
    )(
        mine.reshape(1).astype(jnp.int32),
        *flat_parts,
        *wout_parts,
        joined,
        ffn_gain.reshape(1, width),
        w_up,
        w_down,
    )
    near = flip(odd, "ffn", 1).astype(F32)
    pieces = {0: kept + near[:, :cols]}
    for j in range(2, groups, 2):
        at = j // 2 * cols
        pieces[j] = even[:, at - cols : at] + near[:, at : at + cols]
    bit = 2
    while bit < groups:
        for j in [j for j in pieces if j & bit]:
            pieces[j ^ bit] = pieces[j ^ bit] + flip(pieces.pop(j).astype(BF16), "ffn", bit).astype(F32)
        bit *= 2
    return pieces[0].astype(BF16)


def solution(mesh):
    in_specs = (
        P("seq", None),
        P("seq", None),
        P("seq"),
        P("seq", None),
        P("ffn", "seq"),
        P(),
        P(None, "ffn"),
        P(None, "ffn"),
        P(None, "ffn"),
        P("ffn"),
        P("ffn", None),
        P(),
        P(None, "ffn"),
        P("ffn", None),
    )
    return jax.shard_map(
        on_device, mesh=mesh, in_specs=in_specs, out_specs=P("seq", "ffn"), check_vma=False
    )
```

time: 246 us -> 93.5 us (0.38)
  blocking collectives: 72.7 us -> 0 us
  waiting for transfers between devices: 94.6 us -> 29.3 us
  matrix products: 34.1 us -> 0 us
  Pallas kernels: 0 us -> 29.6 us
  starting transfers between devices: 5.86 us -> 21.9 us
  other arithmetic: 19.6 us -> 4.27 us
  between operations: 14 us -> 0.12 us
  local copies, waits for them, and re-layouts: 4.18 us -> 7.66 us
    psum x1 -> x0, waiting for transfers between devices: 48.8 us -> none  [on_device(): lax.psum(projected.astype(jnp.bfloat16), 'ffn').astype(jnp.float32)]
    dot_general x9 -> x0, matrix products: 34.1 us -> none  [the longest x1 9.22 us: on_device(): jnp.einsum('hst,thd->shd', mixing, value_rows, preferred_element_type=jnp...]
    all_gather x1 -> x0, blocking collectives: 31.5 us -> none  [prefix_2(): lax.all_gather(part.astype(kind), axis)]
    reduce_scatter x1 -> x0, waiting for transfers between devices: 31.4 us -> none  [on_device(): lax.psum_scatter(jnp.dot(expanded, w_down, preferred_element_type=jnp.flo...]
    pallas_call x0 -> x6, Pallas kernels: none -> 29.6 us  [the longest x1 8.56 us: on_device(): pl.pallas_call(functools.partial(ffn_kernel, groups), out_shape=(shaped((...]
    all_to_all x1 -> x0, blocking collectives: 21.7 us -> none  [on_device(): lax.all_to_all(outgoing.reshape(seq_count, capacity, column_share), 'seq'...]
    ppermute x0 -> x8, waiting for transfers between devices: none -> 20.5 us  [flip(): return lax.ppermute(array, axis, [(i, i ^ bit) for i in range(size)])]
    unnamed x1 -> x0, blocking collectives: 19.5 us -> none
  transfers between devices with their start and end apart: 4 -> 11, of which waited for: 3 -> 7; matrix products, arithmetic and copies ran while one was open for 2% -> 5% of each run, Pallas kernels for 0% -> 15%
where the time goes in v1:
time: 93.5 us; the launch traced here: 92.8 us
  Pallas kernels  29.6 us (32%)
  waiting for transfers between devices  29.3 us (31%)
  starting transfers between devices  21.9 us (23%)
  local copies, waits for them, and re-layouts  7.66 us (8%)
  other arithmetic  4.27 us (5%)
    ppermute x8, waiting for transfers between devices, flip(): return lax.ppermute(array, axis, [(i, i ^ bit) for i in range(size)])  20.5 us
    all_to_all x3, starting transfers between devices, exchange(): return lax.all_to_all(array, 'seq', split_axis=0, concat_axis=0, tiled=True)  17.1 us
    all_to_all x3, waiting for transfers between devices, exchange(): return lax.all_to_all(array, 'seq', split_axis=0, concat_axis=0, tiled=True)  8.81 us
    pallas_call x1, Pallas kernels, on_device(): pl.pallas_call(functools.partial(ffn_kernel, groups), out_shape=(shaped((...  8.56 us
    pallas_call x1, Pallas kernels, on_device(): pl.pallas_call(functools.partial(pre_kernel, cap, blocks), out_shape=(sha...  5.67 us
    pallas_call x1, Pallas kernels, on_device(): pl.pallas_call(functools.partial(state_kernel, cap, blocks, hd), out_shap...  5.11 us
    ppermute x8, starting transfers between devices, flip(): return lax.ppermute(array, axis, [(i, i ^ bit) for i in range(size)])  4.77 us
    pallas_call x1, Pallas kernels, on_device(): pl.pallas_call(functools.partial(inside_kernel, cap, blocks, hd), out_sha...  4.59 us
  transfers between devices with their start and end apart: 11, of which 7 were waited for; matrix products, arithmetic and copies ran while one was open for 5% of the time, Pallas kernels for 15%

profile of v1, /device:TPU:0, one launch (start us, length us, event | category | flops | bytes accessed | tf_op | source)
XLA Modules:
  0.0 92.8 jit_solution(15286007451394688254)
XLA Ops:
  0.0 0.8 bitcast_reduce_fusion
  0.8 0.1 copy.16
  0.9 1.3 %pad_maximum_fusion = f32[8,4,136]{2,1,0:T(4,128)} fusion(f32[8,4,8]{2,1,0:T(4,128)S(1)} %broadcast_in_dim.23, f32[8,4,128]{2,1,0:T(4,128)} %bitcast.9), kind=kLoop, calls=%fused_computation.5 | loop fusion | flops 4352 | bytes 34816 | tf_op jit(solution)/shard_map/concatenate | solution.py:263
  2.2 7.3 %all-to-all-start = ((f32[8,4,136]{2,1,0:T(4,128)}), f32[8,4,136]{2,1,0:T(4,128)S(1)}, u32[]{:S(2)}, u32[]{:S(2)}) async-start(f32[8,4,136]{2,1,0:T(4,128)} %pad_maximum_fusion), calls=%async_computation | async-start | bytes 65536 | tf_op jit(solution)/shard_map/all_to_all | solution.py:231
  9.5 1.3 %reshape.34.gain = bf16[1,1024]{1,0:T(2,128)(2,1)} reshape(bf16[1024]{0:T(1024)(128)(2,1)} %param.19) | data formatting | bytes 4096 | tf_op jit(solution)/shard_map/reshape | solution.py:290
  10.8 5.7 %pre.1 = (bf16[512,1024]{1,0:T(8,128)(2,1)}, bf16[512,256]{1,0:T(8,128)(2,1)}, bf16[512,256]{1,0:T(8,128)(2,1)}, bf16[512,256]{1,0:T(8,128)(2,1)}, bf16[1024,1024]{1,0:T(8,128)(2,1)}) custom-call(bf16[512,1024]{1,0:T(8,128)(2,1)} %cf.1, bf16[64,1024]{1,0:T(8,128)(2,1)} %pf.1, s32[1,512]{1,0:T(1,128)} %bitcast.14, s32[1,512]{1,0:T(1,128)} %bitcast.10, ...), custom_call_target="tpu_custom_call" | custom-call | tf_op jit(solution)/shard_map/pre/pallas_call | solution.py:273
  16.5 0.0 all-to-all-done.gates
  16.5 0.6 copy-done.7
  17.1 5.1 %state.1 = (bf16[8,64,256]{2,1,0:T(8,128)(2,1)}, f32[512,256]{1,0:T(8,128)}) custom-call(bf16[1024,1024]{1,0:T(8,128)(2,1)} %get-tuple-element.15.taken, f32[8,4,136]{2,1,0:T(4,128)} %copy-done.7, bf16[512,256]{1,0:T(8,128)(2,1)} %get-tuple-element.16.k, bf16[512,256]{1,0:T(8,128)(2,1)} %get-tuple-element.17.v, s32[1,512]{1,0:T(1,128)} %bitcast.11), custom_call_target="tpu_custom_call" | custom-call | tf_op jit(solution)/shard_map/state/pallas_call | solution.py:296
  22.2 6.1 %all-to-all-start.1 = ((bf16[8,64,256]{2,1,0:T(8,128)(2,1)}), bf16[8,64,256]{2,1,0:T(8,128)(2,1)S(1)}, u32[]{:S(2)}, u32[]{:S(2)}) async-start(bf16[8,64,256]{2,1,0:T(8,128)(2,1)} %get-tuple-element.18), calls=%async_computation.1 | async-start | bytes 524288 | tf_op jit(solution)/shard_map/all_to_all | solution.py:231
  28.3 0.1 broadcast_in_dim.24
  28.4 0.7 reshape.36.decay
  29.1 7.7 %all-to-all-done.1.states = bf16[8,64,256]{2,1,0:T(8,128)(2,1)S(1)} async-done(((bf16[8,64,256]{2,1,0:T(8,128)(2,1)}), bf16[8,64,256]{2,1,0:T(8,128)(2,1)S(1)}, u32[]{:S(2)}, u32[]{:S(2)}) %all-to-all-start.1) | async-done | bytes 262176 | tf_op jit(solution)/shard_map/all_to_all | solution.py:231
  36.8 0.7 copy-done.1
  37.5 1.8 %combine.1 = bf16[8,128,256]{2,1,0:T(8,128)(2,1)} custom-call(bf16[8,64,256]{2,1,0:T(8,128)(2,1)} %copy-done.1, f32[8,256]{1,0:T(8,128)} %reshape.36.decay), custom_call_target="tpu_custom_call" | custom-call | tf_op jit(solution)/shard_map/combine/pallas_call | solution.py:314
  39.3 3.7 %all-to-all-start.2 = ((bf16[8,128,256]{2,1,0:T(8,128)(2,1)}), bf16[8,128,256]{2,1,0:T(8,128)(2,1)S(1)}, u32[]{:S(2)}, u32[]{:S(2)}) async-start(bf16[8,128,256]{2,1,0:T(8,128)(2,1)} %combine.1), calls=%async_computation.2 | async-start | bytes 1048576 | tf_op jit(solution)/shard_map/all_to_all | solution.py:231
  43.0 1.6 %collective-permute-start.4 = (bf16[256,1024]{1,0:T(8,128)(2,1)S(1)}, bf16[256,1024]{1,0:T(8,128)(2,1)S(1)}, u32[]{:S(2)}, u32[]{:S(2)}) collective-permute-start(bf16[256,1024]{1,0:T(8,128)(2,1)S(1)} %copy-done.3), channel_id=1, source_target_pairs={{0,2},{1,3},{2,0},{3,1},{4,6},{5,7},{6,4},{7,5},{8,10},{9,11},{10,... | collective-permute-start | bytes 1572872 | tf_op jit(solution)/shard_map/ppermute | solution.py:212
  44.6 0.0 collective-permute-start.3
  44.6 0.6 reshape.39.gain
  45.2 0.1 slice_reduce_fusion
  45.3 0.1 broadcast_in_dim.27
  45.4 0.7 reshape.37.lead
  46.1 0.1 broadcast_in_dim.28
  46.1 0.7 reshape.38.whole
  46.8 4.6 %inside.1 = f32[512,256]{1,0:T(8,128)} custom-call(bf16[512,256]{1,0:T(8,128)(2,1)} %get-tuple-element.19.q, bf16[512,256]{1,0:T(8,128)(2,1)} %get-tuple-element.16.k, bf16[512,256]{1,0:T(8,128)(2,1)} %get-tuple-element.17.v, bf16[1024,1024]{1,0:T(8,128)(2,1)} %get-tuple-element.15.taken, f32[8,4,136]{2,1,0:T(4,128)} %copy-done.7, ...), custom_call_target="tpu_custom_call" | custom-call | tf_op jit(solution)/shard_map/inside/pallas_call | solution.py:305
  51.4 4.4 %collective-permute-done.4.refs_6_ = bf16[256,1024]{1,0:T(8,128)(2,1)S(1)} collective-permute-done((bf16[256,1024]{1,0:T(8,128)(2,1)S(1)}, bf16[256,1024]{1,0:T(8,128)(2,1)S(1)}, u32[]{:S(2)}, u32[]{:S(2)}) %collective-permute-start.4) | collective-permute-done | bytes 524320 | tf_op jit(solution)/shard_map/ppermute | solution.py:212
  55.8 0.0 collective-permute-start.5
  55.8 1.1 %all-to-all-done.2.back = bf16[8,128,256]{2,1,0:T(8,128)(2,1)S(1)} async-done(((bf16[8,128,256]{2,1,0:T(8,128)(2,1)}), bf16[8,128,256]{2,1,0:T(8,128)(2,1)S(1)}, u32[]{:S(2)}, u32[]{:S(2)}) %all-to-all-start.2) | async-done | bytes 524320 | tf_op jit(solution)/shard_map/all_to_all | solution.py:231
  56.9 0.8 copy-done
  57.7 3.8 %outside.1.refs_0_ = bf16[512,256]{1,0:T(8,128)(2,1)} custom-call(bf16[8,128,256]{2,1,0:T(8,128)(2,1)} %copy-done, f32[8,256]{1,0:T(8,128)} %reshape.37.lead, f32[8,256]{1,0:T(8,128)} %reshape.38.whole, bf16[512,256]{1,0:T(8,128)(2,1)} %get-tuple-element.19.q, s32[1,512]{1,0:T(1,128)} %bitcast.13, f32[512,256]{1,0:T(8,128)} %get-tuple-element.20.c_lanes, ...), custom_call_target="tpu_custom_call" | custom-call | tf_op jit(solution)/shard_map/outside/pallas_call | solution.py:326
  61.5 1.5 %collective-permute-start.1 = (bf16[512,256]{1,0:T(8,128)(2,1)}, bf16[512,256]{1,0:T(8,128)(2,1)S(1)}, u32[]{:S(2)}, u32[]{:S(2)}) collective-permute-start(bf16[512,256]{1,0:T(8,128)(2,1)} %outside.1.refs_0_), channel_id=1, source_target_pairs={{0,2},{1,3},{2,0},{3,1},{4,6},{5,7},{6,4},{7,5},{8,10},{9,11},{10,... | collective-permute-start | bytes 786440 | tf_op jit(solution)/shard_map/ppermute | solution.py:212
  63.0 6.4 %collective-permute-done.1.refs_2_ = bf16[512,256]{1,0:T(8,128)(2,1)S(1)} collective-permute-done((bf16[512,256]{1,0:T(8,128)(2,1)}, bf16[512,256]{1,0:T(8,128)(2,1)S(1)}, u32[]{:S(2)}, u32[]{:S(2)}) %collective-permute-start.1) | collective-permute-done | bytes 262176 | tf_op jit(solution)/shard_map/ppermute | solution.py:212
  69.4 0.0 collective-permute-start.2
  69.4 0.6 reshape.40.refs_9_
  70.0 0.0 collective-permute-done.refs_1_
  70.0 0.0 copy-start.10
  70.0 0.9 collective-permute-done.2.refs_3_
  70.9 0.1 copy-done.6
  71.0 0.0 copy-done.10
  71.1 0.6 copy-done.11
  71.6 8.6 %ffn.1 = (f32[512,256]{1,0:T(8,128)}, f32[512,256]{1,0:T(8,128)}, bf16[512,512]{1,0:T(8,128)(2,1)}) custom-call(s32[1]{0:T(128)} %bitcast.index, bf16[512,256]{1,0:T(8,128)(2,1)} %outside.1.refs_0_, bf16[512,256]{1,0:T(8,128)(2,1)} %copy-done.10, bf16[512,256]{1,0:T(8,128)(2,1)} %copy-done.9, bf16[512,256]{1,0:T(8,128)(2,1)} %copy-done.11, ...), custom_call_target="tpu_custom_call" | custom-call | tf_op jit(solution)/shard_map/ffn/pallas_call | solution.py:340
  80.2 0.2 collective-permute-start.6
  80.3 2.0 %collective-permute-done.6 = bf16[512,512]{1,0:T(8,128)(2,1)S(1)} collective-permute-done((bf16[512,512]{1,0:T(8,128)(2,1)}, bf16[512,512]{1,0:T(8,128)(2,1)S(1)}, u32[]{:S(2)}, u32[]{:S(2)}) %collective-permute-start.6) | collective-permute-done | bytes 524320 | tf_op jit(solution)/shard_map/ppermute | solution.py:212
  82.3 0.1 convert_element_type.12
  82.4 1.1 %fusion = bf16[512,256]{1,0:T(8,128)(2,1)S(1)} fusion(f32[512,256]{1,0:T(8,128)} %get-tuple-element.24, f32[512,512]{1,0:T(8,128)S(1)} %convert_element_type.12), kind=kLoop, calls=%fused_computation.1 | loop fusion | flops 262144 | bytes 1310720 | tf_op jit(solution)/shard_map/convert_element_type | solution.py:368
  83.5 1.6 %collective-permute-start.7 = (bf16[512,256]{1,0:T(8,128)(2,1)S(1)}, bf16[512,256]{1,0:T(8,128)(2,1)S(1)}, u32[]{:S(2)}, u32[]{:S(2)}) collective-permute-start(bf16[512,256]{1,0:T(8,128)(2,1)S(1)} %fusion), channel_id=1, source_target_pairs={{0,2},{1,3},{2,0},{3,1},{4,6},{5,7},{6,4},{7,5},{8,10},{9,11},{10,... | collective-permute-start | bytes 786440 | tf_op jit(solution)/shard_map/ppermute | solution.py:212
  85.1 6.9 %collective-permute-done.7 = bf16[512,256]{1,0:T(8,128)(2,1)S(1)} collective-permute-done((bf16[512,256]{1,0:T(8,128)(2,1)S(1)}, bf16[512,256]{1,0:T(8,128)(2,1)S(1)}, u32[]{:S(2)}, u32[]{:S(2)}) %collective-permute-start.7) | collective-permute-done | bytes 262176 | tf_op jit(solution)/shard_map/ppermute | solution.py:212
  92.0 0.8 fusion.2
  (29 shorter events, 0.1 us)
Async XLA Ops:
  2.2 14.3 %all-to-all-start = ((f32[8,4,136]{2,1,0:T(4,128)}), f32[8,4,136]{2,1,0:T(4,128)S(1)}, u32[]{:S(2)}, u32[]{:S(2)}) async-start(f32[8,4,136]{2,1,0:T(4,128)} %pad_maximum_fusion), calls=%async_computation | async-start | bytes 65536 | tf_op jit(solution)/shard_map/all_to_all | solution.py:231
  16.5 0.6 copy-start.7
  17.1 25.9 %copy-start.3 = (bf16[256,1024]{1,0:T(8,128)(2,1)S(1)}, bf16[256,1024]{1,0:T(8,128)(2,1)}, u32[]{:S(2)}) copy-start(bf16[256,1024]{1,0:T(8,128)(2,1)} %refs_4_.1) | copy-start | bytes 1572868
  17.1 27.5 %copy-start.13 = (bf16[256]{0:T(256)(128)(2,1)S(1)}, bf16[256]{0:T(256)(128)(2,1)}, u32[]{:S(2)}) copy-start(bf16[256]{0:T(256)(128)(2,1)} %param.23) | copy-start | bytes 1540
  22.2 23.0 %copy-start.8 = (f32[8,4,136]{2,1,0:T(4,128)S(1)}, f32[8,4,136]{2,1,0:T(4,128)}, u32[]{:S(2)}) copy-start(f32[8,4,136]{2,1,0:T(4,128)} %copy-done.7) | copy-start | bytes 52228
  22.2 14.6 %all-to-all-start.1 = ((bf16[8,64,256]{2,1,0:T(8,128)(2,1)}), bf16[8,64,256]{2,1,0:T(8,128)(2,1)S(1)}, u32[]{:S(2)}, u32[]{:S(2)}) async-start(bf16[8,64,256]{2,1,0:T(8,128)(2,1)} %get-tuple-element.18), calls=%async_computation.1 | async-start | bytes 524288 | tf_op jit(solution)/shard_map/all_to_all | solution.py:231
  36.8 0.7 copy-start.1
  39.3 17.5 %all-to-all-start.2 = ((bf16[8,128,256]{2,1,0:T(8,128)(2,1)}), bf16[8,128,256]{2,1,0:T(8,128)(2,1)S(1)}, u32[]{:S(2)}, u32[]{:S(2)}) async-start(bf16[8,128,256]{2,1,0:T(8,128)(2,1)} %combine.1), calls=%async_computation.2 | async-start | bytes 1048576 | tf_op jit(solution)/shard_map/all_to_all | solution.py:231
  43.0 12.8 %collective-permute-start.4 = (bf16[256,1024]{1,0:T(8,128)(2,1)S(1)}, bf16[256,1024]{1,0:T(8,128)(2,1)S(1)}, u32[]{:S(2)}, u32[]{:S(2)}) collective-permute-start(bf16[256,1024]{1,0:T(8,128)(2,1)S(1)} %copy-done.3), channel_id=1, source_target_pairs={{0,2},{1,3},{2,0},{3,1},{4,6},{5,7},{6,4},{7,5},{8,10},{9,11},{10,... | collective-permute-start | bytes 1572872 | tf_op jit(solution)/shard_map/ppermute | solution.py:212
  44.6 25.4 %collective-permute-start.3 = (bf16[256,1024]{1,0:T(8,128)(2,1)S(1)}, bf16[256,1024]{1,0:T(8,128)(2,1)S(1)}, u32[]{:S(2)}, u32[]{:S(2)}) collective-permute-start(bf16[256,1024]{1,0:T(8,128)(2,1)S(1)} %copy-done.3), channel_id=1, source_target_pairs={{0,1},{1,0},{2,3},{3,2},{4,5},{5,4},{6,7},{7,6},{8,9},{9,8},{10,11... | collective-permute-start | bytes 1572872 | tf_op jit(solution)/shard_map/ppermute | solution.py:212
  46.8 22.6 %copy-start.12 = (bf16[1024]{0:T(1024)(128)(2,1)S(1)}, bf16[1024]{0:T(1024)(128)(2,1)}, u32[]{:S(2)}) copy-start(bf16[1024]{0:T(1024)(128)(2,1)} %param.25) | copy-start | bytes 6148
  55.8 15.1 %copy-start.4 = (bf16[256,1024]{1,0:T(8,128)(2,1)}, bf16[256,1024]{1,0:T(8,128)(2,1)S(1)}, u32[]{:S(2)}) copy-start(bf16[256,1024]{1,0:T(8,128)(2,1)S(1)} %collective-permute-done.4.refs_6_) | copy-start | bytes 1572868
  55.8 14.2 %collective-permute-start.5 = (bf16[256,1024]{1,0:T(8,128)(2,1)S(1)}, bf16[256,1024]{1,0:T(8,128)(2,1)S(1)}, u32[]{:S(2)}, u32[]{:S(2)}) collective-permute-start(bf16[256,1024]{1,0:T(8,128)(2,1)S(1)} %collective-permute-done.4.refs_6_), channel_id=1, source_target_pairs={{0,1},{1,0},{2,3},{3,2},{4,5},{5,4},{6,7},{7,6},{8,9},{9,8},{10,11... | collective-permute-start | bytes 1572872 | tf_op jit(solution)/shard_map/ppermute | solution.py:212
  56.9 0.8 copy-start
  61.5 7.9 %collective-permute-start.1 = (bf16[512,256]{1,0:T(8,128)(2,1)}, bf16[512,256]{1,0:T(8,128)(2,1)S(1)}, u32[]{:S(2)}, u32[]{:S(2)}) collective-permute-start(bf16[512,256]{1,0:T(8,128)(2,1)} %outside.1.refs_0_), channel_id=1, source_target_pairs={{0,2},{1,3},{2,0},{3,1},{4,6},{5,7},{6,4},{7,5},{8,10},{9,11},{10,... | collective-permute-start | bytes 786440 | tf_op jit(solution)/shard_map/ppermute | solution.py:212
  63.0 7.0 %collective-permute-start = (bf16[512,256]{1,0:T(8,128)(2,1)}, bf16[512,256]{1,0:T(8,128)(2,1)S(1)}, u32[]{:S(2)}, u32[]{:S(2)}) collective-permute-start(bf16[512,256]{1,0:T(8,128)(2,1)} %outside.1.refs_0_), channel_id=1, source_target_pairs={{0,1},{1,0},{2,3},{3,2},{4,5},{5,4},{6,7},{7,6},{8,9},{9,8},{10,11... | collective-permute-start | bytes 786440 | tf_op jit(solution)/shard_map/ppermute | solution.py:212
  69.4 1.5 %copy-start.9 = (bf16[512,256]{1,0:T(8,128)(2,1)}, bf16[512,256]{1,0:T(8,128)(2,1)S(1)}, u32[]{:S(2)}) copy-start(bf16[512,256]{1,0:T(8,128)(2,1)S(1)} %collective-permute-done.1.refs_2_) | copy-start | bytes 786436
  69.4 1.5 %collective-permute-start.2 = (bf16[512,256]{1,0:T(8,128)(2,1)S(1)}, bf16[512,256]{1,0:T(8,128)(2,1)S(1)}, u32[]{:S(2)}, u32[]{:S(2)}) collective-permute-start(bf16[512,256]{1,0:T(8,128)(2,1)S(1)} %collective-permute-done.1.refs_2_), channel_id=1, source_target_pairs={{0,1},{1,0},{2,3},{3,2},{4,5},{5,4},{6,7},{7,6},{8,9},{9,8},{10,11... | collective-permute-start | bytes 786440 | tf_op jit(solution)/shard_map/ppermute | solution.py:212
  70.0 0.9 copy-start.5
  70.0 1.0 %copy-start.6 = (bf16[256,1024]{1,0:T(8,128)(2,1)}, bf16[256,1024]{1,0:T(8,128)(2,1)S(1)}, u32[]{:S(2)}) copy-start(bf16[256,1024]{1,0:T(8,128)(2,1)S(1)} %collective-permute-done.5.refs_7_) | copy-start | bytes 1572868
  70.0 1.0 %copy-start.10 = (bf16[512,256]{1,0:T(8,128)(2,1)}, bf16[512,256]{1,0:T(8,128)(2,1)S(1)}, u32[]{:S(2)}) copy-start(bf16[512,256]{1,0:T(8,128)(2,1)S(1)} %collective-permute-done.refs_1_) | copy-start | bytes 786436
  70.9 0.7 copy-start.11
  80.2 11.8 %copy-start.2 = (f32[512,256]{1,0:T(8,128)S(1)}, f32[512,256]{1,0:T(8,128)}, u32[]{:S(2)}) copy-start(f32[512,256]{1,0:T(8,128)} %get-tuple-element.22) | copy-start | bytes 1572868
  80.2 2.1 %collective-permute-start.6 = (bf16[512,512]{1,0:T(8,128)(2,1)}, bf16[512,512]{1,0:T(8,128)(2,1)S(1)}, u32[]{:S(2)}, u32[]{:S(2)}) collective-permute-start(bf16[512,512]{1,0:T(8,128)(2,1)} %get-tuple-element.23), channel_id=1, source_target_pairs={{0,1},{1,0},{2,3},{3,2},{4,5},{5,4},{6,7},{7,6},{8,9},{9,8},{10,11... | collective-permute-start | bytes 1572872 | tf_op jit(solution)/shard_map/ppermute | solution.py:212
  83.5 8.4 %collective-permute-start.7 = (bf16[512,256]{1,0:T(8,128)(2,1)S(1)}, bf16[512,256]{1,0:T(8,128)(2,1)S(1)}, u32[]{:S(2)}, u32[]{:S(2)}) collective-permute-start(bf16[512,256]{1,0:T(8,128)(2,1)S(1)} %fusion), channel_id=1, source_target_pairs={{0,2},{1,3},{2,0},{3,1},{4,6},{5,7},{6,4},{7,5},{8,10},{9,11},{10,... | collective-permute-start | bytes 786440 | tf_op jit(solution)/shard_map/ppermute | solution.py:212

commit v2 on v1

v2 whole, which is shorter than its diff:
```python
import functools

import jax
import jax.numpy as jnp
from jax import lax
from jax.experimental import pallas as pl
from jax.experimental.pallas import tpu as pltpu
from jax.sharding import PartitionSpec as P


EPSILON = 1e-05
F32 = jnp.float32
BF16 = jnp.bfloat16
LANES = 128
NT = (((1,), (1,)), ((), ()))
TN = (((0,), (0,)), ((), ()))
VMEM = pl.BlockSpec(memory_space=pltpu.VMEM)
HBM = pl.BlockSpec(memory_space=pltpu.HBM)


def split3(values):
    high = values.astype(BF16)
    rest = values - high.astype(F32)
    middle = rest.astype(BF16)
    low = (rest - middle.astype(F32)).astype(BF16)
    return high, middle, low


def dot(a, b):
    return jnp.dot(a, b, preferred_element_type=F32)


def iota(shape, dim):
    return lax.broadcasted_iota(jnp.int32, shape, dim)


def row_norm(values, scales):
    return values * lax.rsqrt(jnp.mean(values * values, axis=-1, keepdims=True) + EPSILON) * scales


def column(row, width=LANES):
    return jnp.broadcast_to(row, (width, row.shape[1])).T


def head_of_lane(shape, hd):
    return iota(shape, len(shape) - 1) // hd


def fetch(pairs, sems):
    copies = [pltpu.make_async_copy(src, dst, sems.at[i]) for i, (src, dst) in enumerate(pairs)]
    for copy in copies:
        copy.start()
    return copies


def pre_kernel(
    cap, blocks, cf, pf, pick, own, gain, wq, wk, wv,
    joined, q, k, v, taken, own_out,
    cf_v, pf_v, pick_v, own_v, gain_v, w_v, joined_v, sems, out_sems,
):
    tokens = cf.shape[0]
    parents = pf.shape[0]
    tile = min(256, tokens)
    starts = range(0, tokens, tile)
    small = fetch(
        [(own, own_v), (pick, pick_v), (pf, pf_v), (gain, gain_v)]
        + [(cf.at[pl.ds(at, tile)], cf_v.at[pl.ds(at, tile)]) for at in starts]
        + [(w, w_v.at[i]) for i, w in enumerate((wq, wk, wv))],
        sems,
    )
    parts, weights = small[4 : 4 + len(starts)], small[4 + len(starts) :]
    small[0].wait()
    owners = own_v[...]
    own_out[...] = owners
    lane = iota((1, blocks * cap), 1)
    lane_owner, lane_rank = lane // cap, lane % cap
    ones = jnp.ones((tokens, LANES), BF16)
    for at in starts:
        rows = pl.ds(at, tile)
        mine = column(own_v[:, rows])
        same = (mine[:, :1] == owners) & (iota((tile, tokens), 0) + at >= iota((tile, tokens), 1))
        count = dot(jnp.where(same, 1.0, 0.0).astype(BF16), ones)
        rank = count[:, :1].astype(jnp.int32) - 1
        kept = (mine[:, :1] == lane_owner) & (lane_rank <= rank)
        taken[rows, :] = jnp.where(kept, 1.0, 0.0).astype(BF16)
    for copy in small[1:4]:
        copy.wait()
    scales = gain_v[...].astype(F32).reshape(1, -1)
    stores = []
    for i, at in enumerate(starts):
        rows = pl.ds(at, tile)
        parts[i].wait()
        chosen = jnp.where(iota((parents, tile), 0) == pick_v[:, rows], 1.0, 0.0).astype(BF16)
        added = lax.dot_general(chosen, pf_v[...], TN, preferred_element_type=F32)
        summed = (cf_v[rows, :].astype(F32) + added).astype(BF16)
        joined_v[rows, :] = summed
        store = pltpu.make_async_copy(joined_v.at[rows], joined.at[rows], out_sems.at[i])
        store.start()
        stores.append(store)
        normed = row_norm(summed.astype(F32), scales).astype(BF16)
        if i == 0:
            for copy in weights:
                copy.wait()
        for j, out in enumerate((q, k, v)):
            out[rows, :] = dot(normed, w_v[j]).astype(BF16)
    for store in stores:
        store.wait()


def gate_rows(gates, blocks):
    if len(gates.shape) == 3:
        rows = jnp.concatenate([gates[o] for o in range(blocks)], axis=1)
    else:
        rows = gates[...]
    heads = rows.shape[0]
    rows = jnp.concatenate([rows, jnp.zeros((8 - heads, rows.shape[1]), F32)], axis=0)
    return jnp.concatenate([part.astype(F32) for part in split3(rows)], axis=0).astype(BF16)


def state_kernel(cap, blocks, hd, taken, gates, k, v, own, states, c_lanes, c_rows, states_v, sems):
    tokens, share = k.shape
    table = gate_rows(gates, blocks)
    summed = lax.dot_general(taken[...], table, NT, preferred_element_type=F32)
    slots = table.shape[1]
    lanes = LANES * pl.cdiv(blocks, LANES)
    chunk = jnp.where(
        iota((slots, lanes), 0) // cap == iota((slots, lanes), 1), 1.0, 0.0
    ).astype(BF16)
    totals = dot(table, chunk)
    totals = jnp.concatenate(
        [part.astype(F32) for part in split3(totals[:8] + totals[8:16] + totals[16:])], axis=0
    ).astype(BF16)
    named = jnp.where(column(own[...])[:, :1] == iota((tokens, lanes), 1), 1.0, 0.0).astype(BF16)
    whole = lax.dot_general(named, totals, NT, preferred_element_type=F32)
    summed = jnp.concatenate([summed, whole], axis=0)
    spread = jnp.where(
        iota((24, share), 0) % 8 == head_of_lane((24, share), hd), 1.0, 0.0
    ).astype(BF16)
    wide = sum(dot(part, spread) for part in split3(summed))
    c_lanes[...] = wide[:tokens]
    turned_c = lax.dot_general(table, taken[...], NT, preferred_element_type=F32)
    c_rows[...] = turned_c[:8] + turned_c[8:16] + turned_c[16:]
    faded = k[...].astype(F32) * jnp.exp(jnp.minimum(wide[tokens:] - wide[:tokens], 0.0))
    turned = faded.astype(BF16).T
    owners = own[...]
    values = v[...]
    lane_head = head_of_lane((hd, share), hd)

    def one(o, nothing):
        masked = jnp.where(owners == o, turned, jnp.zeros_like(turned))
        full = dot(masked, values)
        packed = jnp.zeros((hd, share), F32)
        for h in range(share // hd):
            packed = jnp.where(lane_head == h, full[h * hd : (h + 1) * hd], packed)
        states_v[o] = packed.astype(BF16)
        pltpu.make_async_copy(states_v.at[o], states.at[o], sems.at[o]).start()
        return nothing

    lax.fori_loop(0, blocks, one, 0, unroll=blocks <= 8)
    for o in range(blocks):
        pltpu.make_async_copy(states_v.at[o], states.at[o], sems.at[o]).wait()


def decay_kernel(cap, blocks, hd, gates, decay, tail, gates_v, sem):
    fetch([(gates, gates_v)], sem)[0].wait()
    slots = gates.shape[1]
    share = decay.shape[1]
    table = gate_rows(gates_v, blocks)
    rows = 8 * pl.cdiv(blocks, 8)
    lane_chunk = iota((rows, slots), 1) // cap
    chunk = iota((rows, slots), 0)
    picked = [lane_chunk == chunk, lane_chunk < chunk, lane_chunk >= 0]
    spread = jnp.where(
        iota((24, share), 0) % 8 == head_of_lane((24, share), hd), 1.0, 0.0
    ).astype(BF16)
    outs = []
    for mask in picked:
        summed = lax.dot_general(
            jnp.where(mask, 1.0, 0.0).astype(BF16), table, NT, preferred_element_type=F32
        )
        outs.append(jnp.exp(sum(dot(part, spread) for part in split3(summed))))
    decay[...] = outs[0]
    for at, value in ((0, outs[1]), (4, outs[2])):
        for i, part in enumerate(split3(value)):
            for b in range(blocks):
                tail[b, at + i : at + i + 1, :] = part[b : b + 1].astype(F32)
    for at in (3, 7):
        for b in range(blocks):
            tail[b, at : at + 1, :] = jnp.zeros((1, share), F32)


def combine_kernel(blocks, hd, states, decay, tail, ordered, back):
    def step(b, carry):
        back[b, :hd, :] = carry.astype(BF16)
        back[b, 2 * hd :, :] = tail[b].astype(BF16)
        return decay[pl.ds(b, 1), :] * carry + states[b].astype(F32)

    total = lax.fori_loop(
        0, blocks, step, jnp.zeros(states.shape[1:], F32), unroll=blocks <= 8
    ).astype(BF16)
    for b in range(blocks):
        back[b, hd : 2 * hd, :] = total


def inside_kernel(hd, q, k, v, c_lanes, c_rows, own, inside):
    tokens, share = q.shape
    heads = share // hd
    tile = min(256, tokens)
    for at in range(0, tokens, tile):
        rows = pl.ds(at, tile)
        reach = at + tile
        mine = column(own[:, rows])[:, :1]
        same = (mine == own[:, :reach]) & (
            iota((tile, reach), 0) + at >= iota((tile, reach), 1)
        )
        queries = q[rows, :]
        keys = k[:reach, :]
        values = v[:reach, :]
        total = jnp.zeros((tile, share), F32)
        for h in range(heads):
            only = head_of_lane((tile, share), hd) == h
            scores = lax.dot_general(
                jnp.where(only, queries, jnp.zeros_like(queries)),
                keys,
                NT,
                preferred_element_type=F32,
            )
            gap = c_lanes[rows, h * hd : h * hd + 1] - c_rows[h : h + 1, :reach]
            decay = jnp.where(same, jnp.exp(jnp.where(same, gap, 0.0)), 0.0)
            mixing = (scores * decay).astype(BF16)
            only = head_of_lane((reach, share), hd) == h
            total += dot(mixing, jnp.where(only, values, jnp.zeros_like(values)))
        inside[rows, :] = total


def outside_kernel(blocks, hd, back, q, own, c_lanes, inside, gain, first, second, wide, table):
    tokens, share = q.shape
    heads = share // hd
    mine = column(own[...])[:, :1]
    queries = q[...]
    block_diagonal = iota((share, share), 0) // hd == iota((share, share), 1) // hd

    def step(o, carry):
        tail = back[o, 2 * hd :, :].astype(F32)
        lead = tail[0:1] + tail[1:2] + tail[2:3]
        whole = tail[4:5] + tail[5:6] + tail[6:7]
        state = back[o, :hd, :].astype(F32) + lead * carry
        stacked = jnp.concatenate([state] * heads, axis=0)
        at = pl.ds(pl.multiple_of(o * share, share), share)
        table[at, :] = jnp.where(block_diagonal, stacked, 0.0).astype(BF16)
        wide[:, at] = jnp.where(mine == o, queries, jnp.zeros_like(queries))
        return whole * carry + back[o, hd : 2 * hd, :].astype(F32)

    lax.fori_loop(0, blocks, step, jnp.zeros((hd, share), F32), unroll=blocks <= 8)
    outside = dot(wide[...], table[...]) * jnp.exp(c_lanes[...])
    combined = inside[...] + outside
    square = combined * combined
    mean = jnp.where(block_diagonal, 1.0 / hd, 0.0).astype(BF16)
    spread = sum(dot(part, mean) for part in split3(square))
    flat = (combined * lax.rsqrt(spread + EPSILON) * gain[...].astype(F32)).astype(BF16)
    first[...] = flat[: tokens // 2]
    second[...] = flat[tokens // 2 :]


def load_kernel(groups, *refs):
    owns, nears, wouts = refs[0:2], refs[2:4], refs[4 : 4 + groups]
    joined, gain, w_up, w_down = refs[4 + groups : 8 + groups]
    hidden, wout_v, scale, up_v, down_v = refs[8 + groups : 13 + groups]
    joined_v, gain_v, near_v, sems = refs[13 + groups :]
    copies = fetch(
        [(wouts[0], near_v.at[0]), (wouts[1], near_v.at[1]), (joined, joined_v), (gain, gain_v)]
        + [(w, wout_v.at[i]) for i, w in enumerate(wouts[2:])]
        + [(w_up, up_v), (w_down, down_v)],
        sems,
    )
    for copy in copies[:4]:
        copy.wait()
    scale[...] = gain_v[...].astype(F32).reshape(1, -1)
    rows = owns[0].shape[0]
    for i in range(2):
        at = pl.ds(i * rows, rows)
        hidden[at, :] = (
            joined_v[at, :].astype(F32)
            + dot(owns[i][...], near_v[0])
            + dot(nears[i][...], near_v[1])
        )
    for copy in copies[4:]:
        copy.wait()


def ffn_kernel(groups, at, *refs):
    flats = refs[: groups - 2]
    hidden_v, wout_v, scale, up_v, down_v, own, even, odd, scratch = refs[groups - 2 :]
    mine = lax.axis_index("ffn")
    rows, cols = own.shape
    hidden = hidden_v[pl.ds(at, rows), :]
    for i, flat in enumerate(flats):
        hidden = hidden + dot(flat[...], wout_v[i])
    scratch[...] = hidden
    second = row_norm(hidden, scale[...]).astype(BF16)
    expanded = jax.nn.gelu(dot(second, up_v[...])).astype(BF16)
    for j in sorted(range(groups), key=lambda j: -(j % 2)):
        target = pl.ds(pl.multiple_of((mine ^ j) * cols, cols), cols)
        piece = dot(expanded, down_v[:, target])
        if j == 0:
            own[...] = piece + scratch[:, target]
        elif j % 2:
            odd[:, pl.ds((j // 2) * cols, cols)] = piece.astype(BF16)
        else:
            even[:, pl.ds((j // 2 - 1) * cols, cols)] = piece


def final_kernel(*refs):
    out = refs[-1]
    for i in range(2):
        own, near, far = refs[3 * i : 3 * i + 3]
        rows, cols = own.shape
        out[pl.ds(i * rows, rows), :] = (
            own[...] + near[:, :cols].astype(F32) + far[...].astype(F32)
        ).astype(BF16)


def flip(array, axis, bit):
    size = lax.axis_size(axis)
    return lax.ppermute(array, axis, [(i, i ^ bit) for i in range(size)])


def gather_flips(array, axis):
    size = lax.axis_size(axis)
    parts = {0: array}
    bit = size // 2
    while bit:
        for k in list(parts):
            parts[k ^ bit] = flip(parts[k], axis, bit)
        bit //= 2
    return [parts[k] for k in range(size)]


def grant(mebibytes):
    return pltpu.CompilerParams(vmem_limit_bytes=mebibytes << 20)


def shaped(shape, dtype):
    return jax.ShapeDtypeStruct(shape, dtype)


def in_hbm(array):
    return pltpu.with_memory_space_constraint(array, pltpu.HBM)


def exchange(array):
    return lax.all_to_all(array, "seq", split_axis=0, concat_axis=0, tiled=True)


def on_device(
    child_feat,
    parent_feat,
    child_parent,
    owner,
    log_gate,
    norm_gain,
    w_query,
    w_key,
    w_value,
    head_gain,
    w_out,
    ffn_gain,
    w_up,
    w_down,
):
    blocks = lax.axis_size("seq")
    groups = lax.axis_size("ffn")
    heads, slots = log_gate.shape
    cap = slots // blocks
    tokens, width = child_feat.shape
    share = w_query.shape[1]
    hd = share // heads
    cols = width // groups

    child_feat, parent_feat, w_query, w_key, w_value, w_up, w_down = map(
        in_hbm, (child_feat, parent_feat, w_query, w_key, w_value, w_up, w_down)
    )
    arrived = exchange(log_gate.reshape(heads, blocks, cap).transpose(1, 0, 2))
    if cap % LANES:
        arrived = arrived.transpose(1, 0, 2).reshape(heads, slots)
    wout_parts = [in_hbm(part) for part in gather_flips(w_out, "ffn")]

    tiles = pl.cdiv(tokens, min(256, tokens))
    joined, q, k, v, taken, own = pl.pallas_call(
        functools.partial(pre_kernel, cap, blocks),
        out_shape=(
            pltpu.HBM((tokens, width), BF16),
            shaped((tokens, share), BF16),
            shaped((tokens, share), BF16),
            shaped((tokens, share), BF16),
            shaped((tokens, slots), BF16),
            shaped((1, tokens), jnp.int32),
        ),
        in_specs=[HBM] * 8,
        out_specs=[HBM] + [VMEM] * 5,
        scratch_shapes=[
            pltpu.VMEM((tokens, width), BF16),
            pltpu.VMEM(parent_feat.shape, BF16),
            pltpu.VMEM((1, tokens), jnp.int32),
            pltpu.VMEM((1, tokens), jnp.int32),
            pltpu.VMEM((width,), BF16),
            pltpu.VMEM((3, width, share), BF16),
            pltpu.VMEM((tokens, width), BF16),
            pltpu.SemaphoreType.DMA((7 + tiles,)),
            pltpu.SemaphoreType.DMA((tiles,)),
        ],
        name="pre",
        compiler_params=grant(20),
    )(
        child_feat,
        parent_feat,
        in_hbm(child_parent.reshape(1, tokens)),
        in_hbm(owner.reshape(1, tokens)),
        in_hbm(norm_gain),
        w_query,
        w_key,
        w_value,
    )

    states, c_lanes, c_rows = pl.pallas_call(
        functools.partial(state_kernel, cap, blocks, hd),
        out_shape=(
            pltpu.HBM((blocks, hd, share), BF16),
            shaped((tokens, share), F32),
            shaped((8, tokens), F32),
        ),
        in_specs=[VMEM] * 5,
        out_specs=[HBM] + [VMEM] * 2,
        scratch_shapes=[
            pltpu.VMEM((blocks, hd, share), BF16),
            pltpu.SemaphoreType.DMA((blocks,)),
        ],
        name="state",
        compiler_params=grant(12),
    )(taken, arrived, k, v, own)
    states = exchange(states)

    inside = pl.pallas_call(
        functools.partial(inside_kernel, hd),
        out_shape=shaped((tokens, share), F32),
        in_specs=[VMEM] * 6,
        out_specs=VMEM,
        name="inside",
        compiler_params=grant(12),
    )(q, k, v, c_lanes, c_rows, own)

    decay, tail = pl.pallas_call(
        functools.partial(decay_kernel, cap, blocks, hd),
        out_shape=(
            shaped((8 * pl.cdiv(blocks, 8), share), F32),
            shaped((blocks, 8, share), F32),
        ),
        in_specs=[HBM],
        out_specs=[VMEM] * 2,
        scratch_shapes=[pltpu.VMEM((heads, slots), F32), pltpu.SemaphoreType.DMA((1,))],
        name="decay",
        compiler_params=grant(8),
    )(log_gate)

    back = pl.pallas_call(
        functools.partial(combine_kernel, blocks, hd),
        out_shape=shaped((blocks, 2 * hd + 8, share), BF16),
        in_specs=[VMEM] * 4,
        out_specs=VMEM,
        name="combine",
        compiler_params=grant(8),
    )(states, decay, tail, inside)
    back = exchange(back)

    flats = pl.pallas_call(
        functools.partial(outside_kernel, blocks, hd),
        out_shape=(shaped((tokens // 2, share), BF16),) * 2,
        in_specs=[VMEM] * 6,
        out_specs=[VMEM] * 2,
        scratch_shapes=[
            pltpu.VMEM((tokens, blocks * share), BF16),
            pltpu.VMEM((blocks * share, share), BF16),
        ],
        name="outside",
        compiler_params=grant(16 if blocks <= 8 else 48),
    )(back, q, own, c_lanes, inside, head_gain.reshape(1, share))

    rows, half = tokens // 2, groups // 2
    parts = [gather_flips(flat, "ffn") for flat in flats]
    load = pl.pallas_call(
        functools.partial(load_kernel, groups),
        out_shape=(
            pltpu.VMEM((tokens, width), F32),
            pltpu.VMEM((groups - 2, share, width), BF16),
            pltpu.VMEM((1, width), F32),
            pltpu.VMEM(w_up.shape, BF16),
            pltpu.VMEM(w_down.shape, BF16),
        ),
        in_specs=[VMEM] * 4 + [HBM] * (groups + 4),
        out_specs=[VMEM] * 5,
        scratch_shapes=[
            pltpu.VMEM((tokens, width), BF16),
            pltpu.VMEM((width,), BF16),
            pltpu.VMEM((2, share, width), BF16),
            pltpu.SemaphoreType.DMA((groups + 4,)),
        ],
        name="load",
        compiler_params=grant(12),
    )
    loaded = load(
        parts[0][0],
        parts[1][0],
        parts[0][1],
        parts[1][1],
        *wout_parts,
        in_hbm(joined),
        in_hbm(ffn_gain),
        w_up,
        w_down,
    )
    finals = []
    for i in range(2):
        kept, even, odd = pl.pallas_call(
            functools.partial(ffn_kernel, groups, i * rows),
            out_shape=(
                shaped((rows, cols), F32),
                shaped((rows, max(half - 1, 1) * cols), F32),
                shaped((rows, half * cols), BF16),
            ),
            in_specs=[VMEM] * (groups + 3),
            out_specs=[VMEM] * 3,
            scratch_shapes=[pltpu.VMEM((rows, width), F32)],
            compiler_params=grant(12),
        )(*parts[i][2:], *loaded)
        near = flip(odd, "ffn", 1)
        pieces = {
            j: (
                even[:, (j // 2 - 1) * cols : j // 2 * cols]
                + near[:, j // 2 * cols : (j // 2 + 1) * cols].astype(F32)
            )
            for j in range(2, groups, 2)
        }
        far = [flip(pieces[j].astype(BF16), "ffn", j) for j in pieces]
        far = far[0] if len(far) == 1 else sum(part.astype(F32) for part in far)
        finals += [kept, near, far]
    return pl.pallas_call(
        final_kernel,
        out_shape=shaped((tokens, cols), BF16),
        in_specs=[VMEM] * 6,
        out_specs=VMEM,
        name="final",
        compiler_params=grant(8),
    )(*finals)


def solution(mesh):
    in_specs = (
        P("seq", None),
        P("seq", None),
        P("seq"),
        P("seq", None),
        P("ffn", "seq"),
        P(),
        P(None, "ffn"),
        P(None, "ffn"),
        P(None, "ffn"),
        P("ffn"),
        P("ffn", None),
        P(),
        P(None, "ffn"),
        P("ffn", None),
    )

    return jax.shard_map(
        on_device, mesh=mesh, in_specs=in_specs, out_specs=P("seq", "ffn"), check_vma=False
    )
```

time: 93.5 us -> 75.2 us (0.80)
  Pallas kernels: 29.6 us -> 19.8 us
  local copies, waits for them, and re-layouts: 7.66 us -> 0.02 us
  other arithmetic: 4.27 us -> 0.06 us
  waiting for transfers between devices: 29.3 us -> 32.6 us
    pallas_call x4 -> x8, Pallas kernels: 22.6 us -> 16 us  [the longest x1 4.24 us: on_device(): pl.pallas_call(functools.partial(pre_kernel, cap, blocks), out_shape=(plt...]
    reshape x5 -> x0, local copies, waits for them, and re-layouts: 3.94 us -> none  [the longest x1 1.27 us: on_device(): norm_gain.reshape(1, width)]
    ppermute x8 -> x13, starting transfers between devices: 4.77 us -> 7.56 us  [flip(): return lax.ppermute(array, axis, [(i, i ^ bit) for i in range(size)])]
    unnamed x28 -> x8, local copies, waits for them, and re-layouts: 2.81 us -> 0.02 us
    all_to_all x3, starting transfers between devices: 17.1 us -> 14.7 us  [exchange(): return lax.all_to_all(array, 'seq', split_axis=0, concat_axis=0, tiled=True)]
    pallas_call x1, Pallas kernels: 5.11 us -> 2.83 us  [on_device(): pl.pallas_call(functools.partial(state_kernel, cap, blocks, hd), out_shap...]
    convert_element_type x3 -> x2, other arithmetic: 2.05 us -> 0.06 us  [on_device(): far = [flip(pieces[j].astype(BF16), 'ffn', j) for j in pieces]]
    ppermute x8 -> x13, waiting for transfers between devices: 20.5 us -> 22.3 us  [flip(): return lax.ppermute(array, axis, [(i, i ^ bit) for i in range(size)])]
  transfers between devices with their start and end apart: 11 -> 16, of which waited for: 7 -> 9; matrix products, arithmetic and copies ran while one was open for 5% -> 0% of each run, Pallas kernels for 15% -> 20%
where the time goes in v2:
time: 75.2 us; the launch traced here: 74.9 us
  waiting for transfers between devices  32.6 us (43%)
  starting transfers between devices  22.3 us (30%)
  Pallas kernels  19.8 us (26%)
    ppermute x13, waiting for transfers between devices, flip(): return lax.ppermute(array, axis, [(i, i ^ bit) for i in range(size)])  22.3 us
    all_to_all x3, starting transfers between devices, exchange(): return lax.all_to_all(array, 'seq', split_axis=0, concat_axis=0, tiled=True)  14.7 us
    all_to_all x3, waiting for transfers between devices, exchange(): return lax.all_to_all(array, 'seq', split_axis=0, concat_axis=0, tiled=True)  10.3 us
    ppermute x13, starting transfers between devices, flip(): return lax.ppermute(array, axis, [(i, i ^ bit) for i in range(size)])  7.56 us
    pallas_call x1, Pallas kernels, on_device(): pl.pallas_call(functools.partial(pre_kernel, cap, blocks), out_shape=(plt...  4.24 us
    pallas_call x2, Pallas kernels, on_device(): pl.pallas_call(functools.partial(ffn_kernel, groups, i * rows), out_shape...  3.84 us
    pallas_call x1, Pallas kernels, on_device(): load(parts[0][0], parts[1][0], parts[0][1], parts[1][1], *wout_parts, in_...  3.28 us
    pallas_call x1, Pallas kernels, on_device(): pl.pallas_call(functools.partial(state_kernel, cap, blocks, hd), out_shap...  2.83 us
  transfers between devices with their start and end apart: 16, of which 9 were waited for; matrix products, arithmetic and copies ran while one was open for 0% of the time, Pallas kernels for 20%

profile of v2, /device:TPU:0, one launch (start us, length us, event | category | flops | bytes accessed | tf_op | source)
XLA Modules:
  0.0 74.9 jit_solution(16620310209452427076)
XLA Ops:
  0.0 7.3 %all-to-all-start = ((f32[8,4,128]{2,1,0:T(4,128)}), f32[8,4,128]{2,1,0:T(4,128)S(1)}, u32[]{:S(2)}, u32[]{:S(2)}) async-start(f32[8,4,128]{2,1,0:T(4,128)} %bitcast.5), calls=%async_computation | async-start | bytes 32768 | tf_op jit(solution)/shard_map/all_to_all | solution.py:352
  7.3 4.2 %pre.1 = (bf16[512,1024]{1,0:T(8,128)(2,1)}, bf16[512,256]{1,0:T(8,128)(2,1)S(1)}, bf16[512,256]{1,0:T(8,128)(2,1)S(1)}, bf16[512,256]{1,0:T(8,128)(2,1)S(1)}, b...) custom-call(bf16[512,1024]{1,0:T(8,128)(2,1)} %cf.1, bf16[64,1024]{1,0:T(8,128)(2,1)} %pf.1, s32[1,512]{1,0:T(1,128)} %bitcast.6, ...), custom_call_target="tpu_custom_call" | custom-call | tf_op jit(solution)/shard_map/pre/pallas_call | solution.py:389
  11.6 2.3 %all-to-all-done.gates = f32[8,4,128]{2,1,0:T(4,128)S(1)} async-done(((f32[8,4,128]{2,1,0:T(4,128)}), f32[8,4,128]{2,1,0:T(4,128)S(1)}, u32[]{:S(2)}, u32[]{:S(2)}) %all-to-all-start) | async-done | bytes 16416 | tf_op jit(solution)/shard_map/all_to_all | solution.py:352
  13.9 2.8 %state.1 = (bf16[8,64,256]{2,1,0:T(8,128)(2,1)}, f32[512,256]{1,0:T(8,128)S(1)}, f32[8,512]{1,0:T(8,128)S(1)}) custom-call(bf16[512,1024]{1,0:T(8,128)(2,1)S(1)} %get-tuple-element.29.taken, f32[8,4,128]{2,1,0:T(4,128)S(1)} %all-to-all-done.gates, bf16[512,256]{1,0:T(8,128)(2,1)S(1)} %get-tuple-element.30.k, bf16[512,256]{1,0:T(8,128)(2,1)S(1)} %get-tuple-element.31.v, ...), custom_call_target="tpu_custom_call" | custom-call | tf_op jit(solution)/shard_map/state/pallas_call | solution.py:425
  16.7 3.7 %all-to-all-start.1 = ((bf16[8,64,256]{2,1,0:T(8,128)(2,1)}), bf16[8,64,256]{2,1,0:T(8,128)(2,1)S(1)}, u32[]{:S(2)}, u32[]{:S(2)}) async-start(bf16[8,64,256]{2,1,0:T(8,128)(2,1)} %get-tuple-element.33), calls=%async_computation.1 | async-start | bytes 524288 | tf_op jit(solution)/shard_map/all_to_all | solution.py:352
  20.4 0.0 copy-done
  20.4 0.7 decay.1
  21.1 0.0 copy-start.1
  21.1 0.0 copy-start.3
  21.1 1.6 %inside.1.ordered = f32[512,256]{1,0:T(8,128)S(1)} custom-call(bf16[512,256]{1,0:T(8,128)(2,1)S(1)} %get-tuple-element.36.q, bf16[512,256]{1,0:T(8,128)(2,1)S(1)} %get-tuple-element.30.k, bf16[512,256]{1,0:T(8,128)(2,1)S(1)} %get-tuple-element.31.v, f32[512,256]{1,0:T(8,128)S(1)} %get-tuple-element.37.c_lanes, f32[8,512]{1,0:T(8,128)S(1)} %get-tuple-element.38.c_rows, ...), custom_call_target="tpu_custom_call" | custom-call | tf_op jit(solution)/shard_map/inside/pallas_call | solution.py:443
  22.7 6.2 %all-to-all-done.1.states = bf16[8,64,256]{2,1,0:T(8,128)(2,1)S(1)} async-done(((bf16[8,64,256]{2,1,0:T(8,128)(2,1)}), bf16[8,64,256]{2,1,0:T(8,128)(2,1)S(1)}, u32[]{:S(2)}, u32[]{:S(2)}) %all-to-all-start.1) | async-done | bytes 262176 | tf_op jit(solution)/shard_map/all_to_all | solution.py:352
  28.9 0.9 %combine.1 = bf16[8,136,256]{2,1,0:T(8,128)(2,1)} custom-call(bf16[8,64,256]{2,1,0:T(8,128)(2,1)S(1)} %all-to-all-done.1.states, f32[8,256]{1,0:T(8,128)S(1)} %get-tuple-element.34.decay, f32[8,8,256]{2,1,0:T(8,128)S(1)} %get-tuple-element.35.tail, f32[512,256]{1,0:T(8,128)S(1)} %inside.1.ordered), custom_call_target="tpu_custom_call" | custom-call | tf_op jit(solution)/shard_map/combine/pallas_call | solution.py:465
  29.8 3.7 %all-to-all-start.2 = ((bf16[8,136,256]{2,1,0:T(8,128)(2,1)}), bf16[8,136,256]{2,1,0:T(8,128)(2,1)S(1)}, u32[]{:S(2)}, u32[]{:S(2)}) async-start(bf16[8,136,256]{2,1,0:T(8,128)(2,1)} %combine.1), calls=%async_computation.2 | async-start | bytes 1114112 | tf_op jit(solution)/shard_map/all_to_all | solution.py:352
  33.5 0.0 copy-done.1
  33.5 1.6 %collective-permute-start.5 = (bf16[256,1024]{1,0:T(8,128)(2,1)S(1)}, bf16[256,1024]{1,0:T(8,128)(2,1)S(1)}, u32[]{:S(2)}, u32[]{:S(2)}) collective-permute-start(bf16[256,1024]{1,0:T(8,128)(2,1)S(1)} %copy-done.1), channel_id=1, source_target_pairs={{0,2},{1,3},{2,0},{3,1},{4,6},{5,7},{6,4},{7,5},{8,10},{9,11},{10,... | collective-permute-start | bytes 1572872 | tf_op jit(solution)/shard_map/ppermute | solution.py:325
  35.1 0.0 collective-permute-start.4
  35.1 11.2 %collective-permute-done.5.refs_6_ = bf16[256,1024]{1,0:T(8,128)(2,1)S(1)} collective-permute-done((bf16[256,1024]{1,0:T(8,128)(2,1)S(1)}, bf16[256,1024]{1,0:T(8,128)(2,1)S(1)}, u32[]{:S(2)}, u32[]{:S(2)}) %collective-permute-start.5) | collective-permute-done | bytes 524320 | tf_op jit(solution)/shard_map/ppermute | solution.py:325
  46.3 0.0 collective-permute-start.6
  46.3 0.0 copy-done.3
  46.3 1.8 %all-to-all-done.2.back = bf16[8,136,256]{2,1,0:T(8,128)(2,1)S(1)} async-done(((bf16[8,136,256]{2,1,0:T(8,128)(2,1)}), bf16[8,136,256]{2,1,0:T(8,128)(2,1)S(1)}, u32[]{:S(2)}, u32[]{:S(2)}) %all-to-all-start.2) | async-done | bytes 557088 | tf_op jit(solution)/shard_map/all_to_all | solution.py:352
  48.1 1.6 %outside.1 = (bf16[256,256]{1,0:T(8,128)(2,1)S(1)}, bf16[256,256]{1,0:T(8,128)(2,1)S(1)}) custom-call(bf16[8,136,256]{2,1,0:T(8,128)(2,1)S(1)} %all-to-all-done.2.back, bf16[512,256]{1,0:T(8,128)(2,1)S(1)} %get-tuple-element.36.q, s32[1,512]{1,0:T(1,128)S(1)} %get-tuple-element.32.own, f32[512,256]{1,0:T(8,128)S(1)} %get-tuple-element.37.c_lanes, ...), custom_call_target="tpu_custom_call" | custom-call | tf_op jit(solution)/shard_map/outside/pallas_call | solution.py:475
  49.7 1.6 %collective-permute-start.9 = (bf16[256,256]{1,0:T(8,128)(2,1)S(1)}, bf16[256,256]{1,0:T(8,128)(2,1)S(1)}, u32[]{:S(2)}, u32[]{:S(2)}) collective-permute-start(bf16[256,256]{1,0:T(8,128)(2,1)S(1)} %get-tuple-element.40.refs_1_), channel_id=1, source_target_pairs={{0,2},{1,3},{2,0},{3,1},{4,6},{5,7},{6,4},{7,5},{8,10},{9,11},{10,... | collective-permute-start | bytes 393224 | tf_op jit(solution)/shard_map/ppermute | solution.py:325
  51.3 0.0 collective-permute-start.2
  51.3 0.5 collective-permute-start.3
  51.8 3.0 %collective-permute-done.9.refs_0_ = bf16[256,256]{1,0:T(8,128)(2,1)S(1)} collective-permute-done((bf16[256,256]{1,0:T(8,128)(2,1)S(1)}, bf16[256,256]{1,0:T(8,128)(2,1)S(1)}, u32[]{:S(2)}, u32[]{:S(2)}) %collective-permute-start.9) | collective-permute-done | bytes 131104 | tf_op jit(solution)/shard_map/ppermute | solution.py:325
  54.7 0.0 collective-permute-start.10
  54.7 0.0 collective-permute-done.4.refs_5_
  54.7 1.5 %collective-permute-start = (bf16[256,256]{1,0:T(8,128)(2,1)S(1)}, bf16[256,256]{1,0:T(8,128)(2,1)S(1)}, u32[]{:S(2)}, u32[]{:S(2)}) collective-permute-start(bf16[256,256]{1,0:T(8,128)(2,1)S(1)} %get-tuple-element.39.refs_0_), channel_id=1, source_target_pairs={{0,2},{1,3},{2,0},{3,1},{4,6},{5,7},{6,4},{7,5},{8,10},{9,11},{10,... | collective-permute-start | bytes 393224 | tf_op jit(solution)/shard_map/ppermute | solution.py:325
  56.2 0.0 collective-permute-done.6.refs_7_
  56.2 0.0 collective-permute-done.2.refs_2_
  56.2 0.0 collective-permute-done.3.refs_3_
  56.2 0.0 copy-done.2
  56.2 3.3 %load.1 = (f32[512,1024]{1,0:T(8,128)S(1)}, bf16[2,256,1024]{2,1,0:T(8,128)(2,1)S(1)}, f32[1,1024]{1,0:T(1,128)S(1)}, bf16[1024,1024]{1,0:T(8,128)(2,1)S(1)}, bf16[1024,1024]{1,0:T(8,128)(2,1)S(1)}) custom-call(bf16[256,256]{1,0:T(8,128)(2,1)S(1)} %get-tuple-element.39.refs_0_, bf16[256,256]{1,0:T(8,128)(2,1)S(1)} %get-tuple-element.40.refs_1_, ...), custom_call_target="tpu_custom_call" | custom-call | tf_op jit(solution)/shard_map/load/pallas_call | solution.py:510
  59.5 0.0 collective-permute-done.10.refs_1_
  59.5 1.9 %shard_map.137 = (f32[256,256]{1,0:T(8,128)S(1)}, f32[256,256]{1,0:T(8,128)S(1)}, bf16[256,512]{1,0:T(8,128)(2,1)S(1)}) custom-call(bf16[256,256]{1,0:T(8,128)(2,1)S(1)} %collective-permute-done.9.refs_0_, bf16[256,256]{1,0:T(8,128)(2,1)S(1)} %collective-permute-done.10.refs_1_, f32[512,1024]{1,0:T(8,128)S(1)} %get-tuple-element.42.refs_2_, ...), custom_call_target="tpu_custom_call" | custom-call | tf_op jit(solution)/shard_map/pallas_call | solution.py:523
  61.5 0.3 collective-permute-start.11
  61.8 0.0 collective-permute-done.refs_0_
  61.8 0.3 collective-permute-start.1
  62.0 1.2 %collective-permute-done.1.refs_1_ = bf16[256,256]{1,0:T(8,128)(2,1)S(1)} collective-permute-done((bf16[256,256]{1,0:T(8,128)(2,1)S(1)}, bf16[256,256]{1,0:T(8,128)(2,1)S(1)}, u32[]{:S(2)}, u32[]{:S(2)}) %collective-permute-start.1) | collective-permute-done | bytes 131104 | tf_op jit(solution)/shard_map/ppermute | solution.py:325
  63.3 1.9 %shard_map.136 = (f32[256,256]{1,0:T(8,128)S(1)}, f32[256,256]{1,0:T(8,128)S(1)}, bf16[256,512]{1,0:T(8,128)(2,1)S(1)}) custom-call(bf16[256,256]{1,0:T(8,128)(2,1)S(1)} %collective-permute-done.refs_0_, bf16[256,256]{1,0:T(8,128)(2,1)S(1)} %collective-permute-done.1.refs_1_, f32[512,1024]{1,0:T(8,128)S(1)} %get-tuple-element.42.refs_2_, ...), custom_call_target="tpu_custom_call" | custom-call | tf_op jit(solution)/shard_map/pallas_call | solution.py:523
  65.2 0.3 collective-permute-start.7
  65.5 0.0 collective-permute-done.11.refs_4_
  65.6 0.6 collective-permute-start.12
  66.1 0.7 collective-permute-done.7.refs_1_
  66.8 0.9 %collective-permute-start.8 = (bf16[256,256]{1,0:T(8,128)(2,1)S(1)}, bf16[256,256]{1,0:T(8,128)(2,1)S(1)}, u32[]{:S(2)}, u32[]{:S(2)}) collective-permute-start(bf16[256,256]{1,0:T(8,128)(2,1)S(1)} %add_convert_fusion.1), channel_id=1, source_target_pairs={{0,2},{1,3},{2,0},{3,1},{4,6},{5,7},{6,4},{7,5},{8,10},{9,11},{10,... | collective-permute-start | bytes 393224 | tf_op jit(solution)/shard_map/ppermute | solution.py:325
  67.8 4.2 %collective-permute-done.12.refs_5_ = bf16[256,256]{1,0:T(8,128)(2,1)S(1)} collective-permute-done((bf16[256,256]{1,0:T(8,128)(2,1)S(1)}, bf16[256,256]{1,0:T(8,128)(2,1)S(1)}, u32[]{:S(2)}, u32[]{:S(2)}) %collective-permute-start.12) | collective-permute-done | bytes 131104 | tf_op jit(solution)/shard_map/ppermute | solution.py:325
  72.0 2.1 %collective-permute-done.8.refs_2_ = bf16[256,256]{1,0:T(8,128)(2,1)S(1)} collective-permute-done((bf16[256,256]{1,0:T(8,128)(2,1)S(1)}, bf16[256,256]{1,0:T(8,128)(2,1)S(1)}, u32[]{:S(2)}, u32[]{:S(2)}) %collective-permute-start.8) | collective-permute-done | bytes 131104 | tf_op jit(solution)/shard_map/ppermute | solution.py:325
  74.1 0.8 %final.1 = bf16[512,256]{1,0:T(8,128)(2,1)} custom-call(f32[256,256]{1,0:T(8,128)S(1)} %get-tuple-element.47.refs_0_, bf16[256,512]{1,0:T(8,128)(2,1)S(1)} %collective-permute-done.7.refs_1_, bf16[256,256]{1,0:T(8,128)(2,1)S(1)} %collective-permute-done.8.refs_2_, f32[256,256]{1,0:T(8,128)S(1)} %get-tuple-element.50.refs_3_, ...), custom_call_target="tpu_custom_call" | custom-call | tf_op jit(solution)/shard_map/final/pallas_call | solution.py:546
  (5 shorter events, 0.1 us)
Async XLA Ops:
  0.0 13.9 %all-to-all-start = ((f32[8,4,128]{2,1,0:T(4,128)}), f32[8,4,128]{2,1,0:T(4,128)S(1)}, u32[]{:S(2)}, u32[]{:S(2)}) async-start(f32[8,4,128]{2,1,0:T(4,128)} %bitcast.5), calls=%async_computation | async-start | bytes 32768 | tf_op jit(solution)/shard_map/all_to_all | solution.py:352
  7.3 13.1 %copy-start = (f32[4,1024]{1,0:T(4,128)S(1)}, f32[4,1024]{1,0:T(4,128)}, u32[]{:S(2)}) copy-start(f32[4,1024]{1,0:T(4,128)} %gates.1) | copy-start | bytes 49156
  16.7 12.2 %all-to-all-start.1 = ((bf16[8,64,256]{2,1,0:T(8,128)(2,1)}), bf16[8,64,256]{2,1,0:T(8,128)(2,1)S(1)}, u32[]{:S(2)}, u32[]{:S(2)}) async-start(bf16[8,64,256]{2,1,0:T(8,128)(2,1)} %get-tuple-element.33), calls=%async_computation.1 | async-start | bytes 524288 | tf_op jit(solution)/shard_map/all_to_all | solution.py:352
  21.1 12.4 %copy-start.1 = (bf16[256,1024]{1,0:T(8,128)(2,1)S(1)}, bf16[256,1024]{1,0:T(8,128)(2,1)}, u32[]{:S(2)}) copy-start(bf16[256,1024]{1,0:T(8,128)(2,1)} %refs_4_.1) | copy-start | bytes 1572868
  21.1 25.2 %copy-start.3 = (bf16[256]{0:T(256)(128)(2,1)S(1)}, bf16[256]{0:T(256)(128)(2,1)}, u32[]{:S(2)}) copy-start(bf16[256]{0:T(256)(128)(2,1)} %param.23) | copy-start | bytes 1540
  29.8 18.2 %all-to-all-start.2 = ((bf16[8,136,256]{2,1,0:T(8,128)(2,1)}), bf16[8,136,256]{2,1,0:T(8,128)(2,1)S(1)}, u32[]{:S(2)}, u32[]{:S(2)}) async-start(bf16[8,136,256]{2,1,0:T(8,128)(2,1)} %combine.1), calls=%async_computation.2 | async-start | bytes 1114112 | tf_op jit(solution)/shard_map/all_to_all | solution.py:352
  33.5 12.7 %collective-permute-start.5 = (bf16[256,1024]{1,0:T(8,128)(2,1)S(1)}, bf16[256,1024]{1,0:T(8,128)(2,1)S(1)}, u32[]{:S(2)}, u32[]{:S(2)}) collective-permute-start(bf16[256,1024]{1,0:T(8,128)(2,1)S(1)} %copy-done.1), channel_id=1, source_target_pairs={{0,2},{1,3},{2,0},{3,1},{4,6},{5,7},{6,4},{7,5},{8,10},{9,11},{10,... | collective-permute-start | bytes 1572872 | tf_op jit(solution)/shard_map/ppermute | solution.py:325
  35.1 19.6 %collective-permute-start.4 = (bf16[256,1024]{1,0:T(8,128)(2,1)S(1)}, bf16[256,1024]{1,0:T(8,128)(2,1)}, u32[]{:S(2)}, u32[]{:S(2)}) collective-permute-start(bf16[256,1024]{1,0:T(8,128)(2,1)S(1)} %copy-done.1), channel_id=1, source_target_pairs={{0,1},{1,0},{2,3},{3,2},{4,5},{5,4},{6,7},{7,6},{8,9},{9,8},{10,11... | collective-permute-start | bytes 1572872 | tf_op jit(solution)/shard_map/ppermute | solution.py:325
  46.3 10.0 %copy-start.2 = (bf16[256,1024]{1,0:T(8,128)(2,1)}, bf16[256,1024]{1,0:T(8,128)(2,1)S(1)}, u32[]{:S(2)}) copy-start(bf16[256,1024]{1,0:T(8,128)(2,1)S(1)} %collective-permute-done.5.refs_6_) | copy-start | bytes 1572868
  46.3 9.9 %collective-permute-start.6 = (bf16[256,1024]{1,0:T(8,128)(2,1)S(1)}, bf16[256,1024]{1,0:T(8,128)(2,1)}, u32[]{:S(2)}, u32[]{:S(2)}) collective-permute-start(bf16[256,1024]{1,0:T(8,128)(2,1)S(1)} %collective-permute-done.5.refs_6_), channel_id=1, source_target_pairs={{0,1},{1,0},{2,3},{3,2},{4,5},{5,4},{6,7},{7,6},{8,9},{9,8},{10,11... | collective-permute-start | bytes 1572872 | tf_op jit(solution)/shard_map/ppermute | solution.py:325
  49.7 5.0 %collective-permute-start.9 = (bf16[256,256]{1,0:T(8,128)(2,1)S(1)}, bf16[256,256]{1,0:T(8,128)(2,1)S(1)}, u32[]{:S(2)}, u32[]{:S(2)}) collective-permute-start(bf16[256,256]{1,0:T(8,128)(2,1)S(1)} %get-tuple-element.40.refs_1_), channel_id=1, source_target_pairs={{0,2},{1,3},{2,0},{3,1},{4,6},{5,7},{6,4},{7,5},{8,10},{9,11},{10,... | collective-permute-start | bytes 393224 | tf_op jit(solution)/shard_map/ppermute | solution.py:325
  51.3 5.0 %collective-permute-start.2 = (bf16[256,256]{1,0:T(8,128)(2,1)S(1)}, bf16[256,256]{1,0:T(8,128)(2,1)S(1)}, u32[]{:S(2)}, u32[]{:S(2)}) collective-permute-start(bf16[256,256]{1,0:T(8,128)(2,1)S(1)} %get-tuple-element.39.refs_0_), channel_id=1, source_target_pairs={{0,1},{1,0},{2,3},{3,2},{4,5},{5,4},{6,7},{7,6},{8,9},{9,8},{10,11... | collective-permute-start | bytes 393224 | tf_op jit(solution)/shard_map/ppermute | solution.py:325
  51.3 5.0 %collective-permute-start.3 = (bf16[256,256]{1,0:T(8,128)(2,1)S(1)}, bf16[256,256]{1,0:T(8,128)(2,1)S(1)}, u32[]{:S(2)}, u32[]{:S(2)}) collective-permute-start(bf16[256,256]{1,0:T(8,128)(2,1)S(1)} %get-tuple-element.40.refs_1_), channel_id=1, source_target_pairs={{0,1},{1,0},{2,3},{3,2},{4,5},{5,4},{6,7},{7,6},{8,9},{9,8},{10,11... | collective-permute-start | bytes 393224 | tf_op jit(solution)/shard_map/ppermute | solution.py:325
  54.7 4.8 %collective-permute-start.10 = (bf16[256,256]{1,0:T(8,128)(2,1)S(1)}, bf16[256,256]{1,0:T(8,128)(2,1)S(1)}, u32[]{:S(2)}, u32[]{:S(2)}) collective-permute-start(bf16[256,256]{1,0:T(8,128)(2,1)S(1)} %collective-permute-done.9.refs_0_), channel_id=1, source_target_pairs={{0,1},{1,0},{2,3},{3,2},{4,5},{5,4},{6,7},{7,6},{8,9},{9,8},{10,11... | collective-permute-start | bytes 393224 | tf_op jit(solution)/shard_map/ppermute | solution.py:325
  54.7 7.1 %collective-permute-start = (bf16[256,256]{1,0:T(8,128)(2,1)S(1)}, bf16[256,256]{1,0:T(8,128)(2,1)S(1)}, u32[]{:S(2)}, u32[]{:S(2)}) collective-permute-start(bf16[256,256]{1,0:T(8,128)(2,1)S(1)} %get-tuple-element.39.refs_0_), channel_id=1, source_target_pairs={{0,2},{1,3},{2,0},{3,1},{4,6},{5,7},{6,4},{7,5},{8,10},{9,11},{10,... | collective-permute-start | bytes 393224 | tf_op jit(solution)/shard_map/ppermute | solution.py:325
  61.5 4.1 %collective-permute-start.11 = (bf16[256,512]{1,0:T(8,128)(2,1)S(1)}, bf16[256,512]{1,0:T(8,128)(2,1)S(1)}, u32[]{:S(2)}, u32[]{:S(2)}) collective-permute-start(bf16[256,512]{1,0:T(8,128)(2,1)S(1)} %get-tuple-element.51), channel_id=1, source_target_pairs={{0,1},{1,0},{2,3},{3,2},{4,5},{5,4},{6,7},{7,6},{8,9},{9,8},{10,11... | collective-permute-start | bytes 786440 | tf_op jit(solution)/shard_map/ppermute | solution.py:325
  61.8 1.5 %collective-permute-start.1 = (bf16[256,256]{1,0:T(8,128)(2,1)S(1)}, bf16[256,256]{1,0:T(8,128)(2,1)S(1)}, u32[]{:S(2)}, u32[]{:S(2)}) collective-permute-start(bf16[256,256]{1,0:T(8,128)(2,1)S(1)} %collective-permute-done.refs_0_), channel_id=1, source_target_pairs={{0,1},{1,0},{2,3},{3,2},{4,5},{5,4},{6,7},{7,6},{8,9},{9,8},{10,11... | collective-permute-start | bytes 393224 | tf_op jit(solution)/shard_map/ppermute | solution.py:325
  65.2 1.6 %collective-permute-start.7 = (bf16[256,512]{1,0:T(8,128)(2,1)S(1)}, bf16[256,512]{1,0:T(8,128)(2,1)S(1)}, u32[]{:S(2)}, u32[]{:S(2)}) collective-permute-start(bf16[256,512]{1,0:T(8,128)(2,1)S(1)} %get-tuple-element.48), channel_id=1, source_target_pairs={{0,1},{1,0},{2,3},{3,2},{4,5},{5,4},{6,7},{7,6},{8,9},{9,8},{10,11... | collective-permute-start | bytes 786440 | tf_op jit(solution)/shard_map/ppermute | solution.py:325
  65.6 6.4 %collective-permute-start.12 = (bf16[256,256]{1,0:T(8,128)(2,1)S(1)}, bf16[256,256]{1,0:T(8,128)(2,1)S(1)}, u32[]{:S(2)}, u32[]{:S(2)}) collective-permute-start(bf16[256,256]{1,0:T(8,128)(2,1)S(1)} %add_convert_fusion), channel_id=1, source_target_pairs={{0,2},{1,3},{2,0},{3,1},{4,6},{5,7},{6,4},{7,5},{8,10},{9,11},{10,... | collective-permute-start | bytes 393224 | tf_op jit(solution)/shard_map/ppermute | solution.py:325
  66.8 7.2 %collective-permute-start.8 = (bf16[256,256]{1,0:T(8,128)(2,1)S(1)}, bf16[256,256]{1,0:T(8,128)(2,1)S(1)}, u32[]{:S(2)}, u32[]{:S(2)}) collective-permute-start(bf16[256,256]{1,0:T(8,128)(2,1)S(1)} %add_convert_fusion.1), channel_id=1, source_target_pairs={{0,2},{1,3},{2,0},{3,1},{4,6},{5,7},{6,4},{7,5},{8,10},{9,11},{10,... | collective-permute-start | bytes 393224 | tf_op jit(solution)/shard_map/ppermute | solution.py:325

commit v3 on v2

--- a/solution.py
+++ b/solution.py
@@ -117,20 +117,34 @@
     return jnp.concatenate([part.astype(F32) for part in split3(rows)], axis=0).astype(BF16)
 
 
-def state_kernel(cap, blocks, hd, taken, gates, k, v, own, states, c_lanes, c_rows, states_v, sems):
+def seat(owner, blocks):
+    half = max(blocks // 2, 1)
+    return owner // half * (8 * pl.cdiv(half, 8)) + owner % half
+
+
+def put_tail(send, decay, at):
+    high = decay.astype(BF16)
+    low = decay - high.astype(F32)
+    send[at:, :] = jnp.concatenate([high.astype(F32), low], axis=0).astype(BF16)
+
+
+def state_kernel(cap, blocks, hd, taken, gates, k, v, own, c_lanes, c_rows, *outs):
     tokens, share = k.shape
+    half = blocks // 2
+    rows = 8 * pl.cdiv(half, 8)
     table = gate_rows(gates, blocks)
+    slots = table.shape[1]
     summed = lax.dot_general(taken[...], table, NT, preferred_element_type=F32)
-    slots = table.shape[1]
-    lanes = LANES * pl.cdiv(blocks, LANES)
+    lanes = LANES * pl.cdiv(2 * rows, LANES)
     chunk = jnp.where(
-        iota((slots, lanes), 0) // cap == iota((slots, lanes), 1), 1.0, 0.0
+        seat(iota((slots, lanes), 0) // cap, blocks) == iota((slots, lanes), 1), 1.0, 0.0
     ).astype(BF16)
     totals = dot(table, chunk)
     totals = jnp.concatenate(
         [part.astype(F32) for part in split3(totals[:8] + totals[8:16] + totals[16:])], axis=0
     ).astype(BF16)
-    named = jnp.where(column(own[...])[:, :1] == iota((tokens, lanes), 1), 1.0, 0.0).astype(BF16)
+    mine = column(seat(own[...], blocks))[:, :1]
+    named = jnp.where(mine == iota((tokens, lanes), 1), 1.0, 0.0).astype(BF16)
     whole = lax.dot_general(named, totals, NT, preferred_element_type=F32)
     summed = jnp.concatenate([summed, whole], axis=0)
     spread = jnp.where(
@@ -142,64 +156,65 @@
     c_rows[...] = turned_c[:8] + turned_c[8:16] + turned_c[16:]
     faded = k[...].astype(F32) * jnp.exp(jnp.minimum(wide[tokens:] - wide[:tokens], 0.0))
     turned = faded.astype(BF16).T
+    decays = jnp.exp(lax.dot_general(totals, spread, TN, preferred_element_type=F32))
     owners = own[...]
     values = v[...]
     lane_head = head_of_lane((hd, share), hd)
-
-    def one(o, nothing):
-        masked = jnp.where(owners == o, turned, jnp.zeros_like(turned))
-        full = dot(masked, values)
-        packed = jnp.zeros((hd, share), F32)
-        for h in range(share // hd):
-            packed = jnp.where(lane_head == h, full[h * hd : (h + 1) * hd], packed)
-        states_v[o] = packed.astype(BF16)
-        pltpu.make_async_copy(states_v.at[o], states.at[o], sems.at[o]).start()
-        return nothing
-
-    lax.fori_loop(0, blocks, one, 0, unroll=blocks <= 8)
-    for o in range(blocks):
-        pltpu.make_async_copy(states_v.at[o], states.at[o], sems.at[o]).wait()
-
-
-def decay_kernel(cap, blocks, hd, gates, decay, tail, gates_v, sem):
-    fetch([(gates, gates_v)], sem)[0].wait()
-    slots = gates.shape[1]
-    share = decay.shape[1]
-    table = gate_rows(gates_v, blocks)
-    rows = 8 * pl.cdiv(blocks, 8)
-    lane_chunk = iota((rows, slots), 1) // cap
-    chunk = iota((rows, slots), 0)
-    picked = [lane_chunk == chunk, lane_chunk < chunk, lane_chunk >= 0]
-    spread = jnp.where(
-        iota((24, share), 0) % 8 == head_of_lane((24, share), hd), 1.0, 0.0
-    ).astype(BF16)
-    outs = []
-    for mask in picked:
-        summed = lax.dot_general(
-            jnp.where(mask, 1.0, 0.0).astype(BF16), table, NT, preferred_element_type=F32
-        )
-        outs.append(jnp.exp(sum(dot(part, spread) for part in split3(summed))))
-    decay[...] = outs[0]
-    for at, value in ((0, outs[1]), (4, outs[2])):
-        for i, part in enumerate(split3(value)):
-            for b in range(blocks):
-                tail[b, at + i : at + i + 1, :] = part[b : b + 1].astype(F32)
-    for at in (3, 7):
-        for b in range(blocks):
-            tail[b, at : at + 1, :] = jnp.zeros((1, share), F32)
-
-
-def combine_kernel(blocks, hd, states, decay, tail, ordered, back):
-    def step(b, carry):
-        back[b, :hd, :] = carry.astype(BF16)
-        back[b, 2 * hd :, :] = tail[b].astype(BF16)
-        return decay[pl.ds(b, 1), :] * carry + states[b].astype(F32)
-
-    total = lax.fori_loop(
-        0, blocks, step, jnp.zeros(states.shape[1:], F32), unroll=blocks <= 8
-    ).astype(BF16)
-    for b in range(blocks):
-        back[b, hd : 2 * hd, :] = total
+    for g in range(2):
+        send, state, decay = outs[3 * g : 3 * g + 3]
+
+        def one(i, nothing):
+            masked = jnp.where(owners == i + g * half, turned, jnp.zeros_like(turned))
+            full = dot(masked, values)
+            packed = jnp.zeros((hd, share), F32)
+            for h in range(share // hd):
+                packed = jnp.where(lane_head == h, full[h * hd : (h + 1) * hd], packed)
+            state[i] = packed
+            send[pl.ds(pl.multiple_of(i * hd, hd), hd), :] = packed.astype(BF16)
+            return nothing
+
+        lax.fori_loop(0, half, one, 0, unroll=blocks <= 8)
+        decay[...] = decays[g * rows : (g + 1) * rows]
+        put_tail(send, decay[...], half * hd)
+
+
+def joined_scan(bit, hd, refs):
+    came, state, decay, prefix, lead = refs
+    half = state.shape[0]
+    rows = decay.shape[0]
+    upper = ((lax.axis_index("seq") & bit) // bit).astype(F32)
+    tail = came[half * hd :, :].astype(F32)
+    theirs_decay = tail[:rows] + tail[rows:]
+    mine_decay = decay[...]
+    past = jnp.ones_like(mine_decay) if lead is None else lead[...]
+    scale_mine = upper + (1.0 - upper) * theirs_decay
+    scale_theirs = upper * mine_decay + (1.0 - upper)
+    add = upper * past
+    pairs = []
+    for i in range(half):
+        theirs = came[i * hd : (i + 1) * hd, :].astype(F32)
+        total = scale_mine[i : i + 1] * state[i] + scale_theirs[i : i + 1] * theirs
+        before = add[i : i + 1] * theirs
+        pairs.append((total, before if prefix is None else prefix[i] + before))
+    return pairs, mine_decay * theirs_decay, past * scale_mine_lead(upper, theirs_decay)
+
+
+def scale_mine_lead(upper, theirs_decay):
+    return upper * theirs_decay + (1.0 - upper)
+
+
+def step_kernel(bit, hd, first, *refs):
+    came, state, decay = refs[:3]
+    prefix, lead = (None, None) if first else refs[3:5]
+    send, state_out, decay_out, prefix_out, lead_out = refs[-5:]
+    pairs, total_decay, total_lead = joined_scan(bit, hd, (came, state, decay, prefix, lead))
+    for i, (total, before) in enumerate(pairs):
+        state_out[i] = total
+        prefix_out[i] = before
+        send[i * hd : (i + 1) * hd, :] = total.astype(BF16)
+    decay_out[...] = total_decay
+    lead_out[...] = total_lead
+    put_tail(send, total_decay, len(pairs) * hd)
 
 
 def inside_kernel(hd, q, k, v, c_lanes, c_rows, own, inside):
@@ -233,25 +248,25 @@
         inside[rows, :] = total
 
 
-def outside_kernel(blocks, hd, back, q, own, c_lanes, inside, gain, first, second, wide, table):
+def outside_kernel(bit, hd, *refs):
+    halves = [refs[5 * g : 5 * g + 5] for g in range(2)]
+    q, own, c_lanes, inside, gain, first, second, wide, table = refs[10:]
     tokens, share = q.shape
     heads = share // hd
     mine = column(own[...])[:, :1]
     queries = q[...]
     block_diagonal = iota((share, share), 0) // hd == iota((share, share), 1) // hd
-
-    def step(o, carry):
-        tail = back[o, 2 * hd :, :].astype(F32)
-        lead = tail[0:1] + tail[1:2] + tail[2:3]
-        whole = tail[4:5] + tail[5:6] + tail[6:7]
-        state = back[o, :hd, :].astype(F32) + lead * carry
-        stacked = jnp.concatenate([state] * heads, axis=0)
-        at = pl.ds(pl.multiple_of(o * share, share), share)
-        table[at, :] = jnp.where(block_diagonal, stacked, 0.0).astype(BF16)
-        wide[:, at] = jnp.where(mine == o, queries, jnp.zeros_like(queries))
-        return whole * carry + back[o, hd : 2 * hd, :].astype(F32)
-
-    lax.fori_loop(0, blocks, step, jnp.zeros((hd, share), F32), unroll=blocks <= 8)
+    carry = jnp.zeros((hd, share), F32)
+    for g in range(2):
+        pairs, whole, lead = joined_scan(bit, hd, halves[g])
+        for i, (total, before) in enumerate(pairs):
+            o = g * len(pairs) + i
+            state = before + lead[i : i + 1] * carry
+            stacked = jnp.concatenate([state] * heads, axis=0)
+            at = pl.ds(o * share, share)
+            table[at, :] = jnp.where(block_diagonal, stacked, 0.0).astype(BF16)
+            wide[:, at] = jnp.where(mine == o, queries, jnp.zeros_like(queries))
+            carry = whole[i : i + 1] * carry + total
     outside = dot(wide[...], table[...]) * jnp.exp(c_lanes[...])
     combined = inside[...] + outside
     square = combined * combined
@@ -422,23 +437,20 @@
         w_value,
     )
 
-    states, c_lanes, c_rows = pl.pallas_call(
+    half = blocks // 2
+    seats = 8 * pl.cdiv(half, 8)
+    sent = shaped((half * hd + 2 * seats, share), BF16)
+    held = shaped((half, hd, share), F32)
+    rate = shaped((seats, share), F32)
+    c_lanes, c_rows, *made = pl.pallas_call(
         functools.partial(state_kernel, cap, blocks, hd),
-        out_shape=(
-            pltpu.HBM((blocks, hd, share), BF16),
-            shaped((tokens, share), F32),
-            shaped((8, tokens), F32),
-        ),
+        out_shape=(shaped((tokens, share), F32), shaped((8, tokens), F32)) + (sent, held, rate) * 2,
         in_specs=[VMEM] * 5,
-        out_specs=[HBM] + [VMEM] * 2,
-        scratch_shapes=[
-            pltpu.VMEM((blocks, hd, share), BF16),
-            pltpu.SemaphoreType.DMA((blocks,)),
-        ],
+        out_specs=[VMEM] * 8,
         name="state",
-        compiler_params=grant(12),
+        compiler_params=grant(12 if blocks <= 8 else 24),
     )(taken, arrived, k, v, own)
-    states = exchange(states)
+    scans = [made[:3], made[3:]]
 
     inside = pl.pallas_call(
         functools.partial(inside_kernel, hd),
@@ -449,41 +461,33 @@
         compiler_params=grant(12),
     )(q, k, v, c_lanes, c_rows, own)
 
-    decay, tail = pl.pallas_call(
-        functools.partial(decay_kernel, cap, blocks, hd),
-        out_shape=(
-            shaped((8 * pl.cdiv(blocks, 8), share), F32),
-            shaped((blocks, 8, share), F32),
-        ),
-        in_specs=[HBM],
-        out_specs=[VMEM] * 2,
-        scratch_shapes=[pltpu.VMEM((heads, slots), F32), pltpu.SemaphoreType.DMA((1,))],
-        name="decay",
-        compiler_params=grant(8),
-    )(log_gate)
-
-    back = pl.pallas_call(
-        functools.partial(combine_kernel, blocks, hd),
-        out_shape=shaped((blocks, 2 * hd + 8, share), BF16),
-        in_specs=[VMEM] * 4,
-        out_specs=VMEM,
-        name="combine",
-        compiler_params=grant(8),
-    )(states, decay, tail, inside)
-    back = exchange(back)
+    bits = [1 << i for i in range(blocks.bit_length() - 1)]
+    for bit in bits:
+        for g in range(2):
+            came = flip(scans[g][0], "seq", bit)
+            if bit == bits[-1]:
+                scans[g] = [came, *scans[g][1:]]
+                continue
+            scans[g] = pl.pallas_call(
+                functools.partial(step_kernel, bit, hd, bit == 1),
+                out_shape=(sent, held, rate, held, rate),
+                in_specs=[VMEM] * len(scans[g]),
+                out_specs=[VMEM] * 5,
+                compiler_params=grant(6 if blocks <= 8 else 24),
+            )(came, *scans[g][1:])
 
     flats = pl.pallas_call(
-        functools.partial(outside_kernel, blocks, hd),
+        functools.partial(outside_kernel, bits[-1], hd),
         out_shape=(shaped((tokens // 2, share), BF16),) * 2,
-        in_specs=[VMEM] * 6,
+        in_specs=[VMEM] * 15,
         out_specs=[VMEM] * 2,
         scratch_shapes=[
             pltpu.VMEM((tokens, blocks * share), BF16),
             pltpu.VMEM((blocks * share, share), BF16),
         ],
         name="outside",
-        compiler_params=grant(16 if blocks <= 8 else 48),
-    )(back, q, own, c_lanes, inside, head_gain.reshape(1, share))
+        compiler_params=grant(12 if blocks <= 8 else 52),
+    )(*scans[0], *scans[1], q, own, c_lanes, inside, head_gain.reshape(1, share))
 
     rows, half = tokens // 2, groups // 2
     parts = [gather_flips(flat, "ffn") for flat in flats]

time: 75.2 us -> 68.2 us (0.907)
  waiting for transfers between devices: 32.6 us -> 28.2 us
  Pallas kernels: 19.8 us -> 18 us
  starting transfers between devices: 22.3 us -> 20.7 us
  local copies, waits for them, and re-layouts: 0.02 us -> 0.82 us
    all_to_all x3 -> x1, starting transfers between devices: 14.7 us -> 5.83 us  [exchange(): return lax.all_to_all(array, 'seq', split_axis=0, concat_axis=0, tiled=True)]
    all_to_all x3 -> x1, waiting for transfers between devices: 10.3 us -> 2.26 us  [exchange(): return lax.all_to_all(array, 'seq', split_axis=0, concat_axis=0, tiled=True)]
    ppermute x13 -> x19, starting transfers between devices: 7.56 us -> 14.9 us  [flip(): return lax.ppermute(array, axis, [(i, i ^ bit) for i in range(size)])]
    ppermute x13 -> x19, waiting for transfers between devices: 22.3 us -> 26 us  [flip(): return lax.ppermute(array, axis, [(i, i ^ bit) for i in range(size)])]
    pallas_call x3 -> x5, Pallas kernels: 3.18 us -> 1.96 us  [the longest x1 1.66 us: on_device(): pl.pallas_call(functools.partial(outside_kernel, bits[-1], hd), out_shape...]
    unnamed x8 -> x10, local copies, waits for them, and re-layouts: 0.02 us -> 0.82 us
  transfers between devices with their start and end apart: 16 -> 20, of which waited for: 9 -> 11; matrix products, arithmetic and copies ran while one was open for 0% -> 0% of each run, Pallas kernels for 20% -> 25%
where the time goes in v3:
time: 68.2 us; the launch traced here: 68 us
  waiting for transfers between devices  28.2 us (41%)
  starting transfers between devices  20.7 us (30%)
  Pallas kernels  18 us (26%)
  local copies, waits for them, and re-layouts  0.82 us (1%)
    ppermute x19, waiting for transfers between devices, flip(): return lax.ppermute(array, axis, [(i, i ^ bit) for i in range(size)])  26 us
    ppermute x19, starting transfers between devices, flip(): return lax.ppermute(array, axis, [(i, i ^ bit) for i in range(size)])  14.9 us
    all_to_all x1, starting transfers between devices, exchange(): return lax.all_to_all(array, 'seq', split_axis=0, concat_axis=0, tiled=True)  5.83 us
    pallas_call x1, Pallas kernels, on_device(): pl.pallas_call(functools.partial(pre_kernel, cap, blocks), out_shape=(plt...  4.29 us
    pallas_call x2, Pallas kernels, on_device(): pl.pallas_call(functools.partial(ffn_kernel, groups, i * rows), out_shape...  3.86 us
    pallas_call x1, Pallas kernels, on_device(): load(parts[0][0], parts[1][0], parts[0][1], parts[1][1], *wout_parts, in_...  3.27 us
    all_to_all x1, waiting for transfers between devices, exchange(): return lax.all_to_all(array, 'seq', split_axis=0, concat_axis=0, tiled=True)  2.26 us
    pallas_call x1, Pallas kernels, on_device(): pl.pallas_call(functools.partial(state_kernel, cap, blocks, hd), out_shap...  2.15 us
  transfers between devices with their start and end apart: 20, of which 11 were waited for; matrix products, arithmetic and copies ran while one was open for 0% of the time, Pallas kernels for 25%

profile of v3, /device:TPU:0, one launch (start us, length us, event | category | flops | bytes accessed | tf_op | source)
XLA Modules:
  0.0 68.0 jit_solution(2988722314392885799)
XLA Ops:
  0.0 3.0 %collective-permute-start.11 = (bf16[256,1024]{1,0:T(8,128)(2,1)}, bf16[256,1024]{1,0:T(8,128)(2,1)S(1)}, u32[]{:S(2)}, u32[]{:S(2)}) collective-permute-start(bf16[256,1024]{1,0:T(8,128)(2,1)} %refs_4_.1), channel_id=1, source_target_pairs={{0,2},{1,3},{2,0},{3,1},{4,6},{5,7},{6,4},{7,5},{8,10},{9,11},{10,... | collective-permute-start | bytes 1572872 | tf_op jit(solution)/shard_map/ppermute | solution.py:340
  3.0 5.8 %all-to-all-start = ((f32[8,4,128]{2,1,0:T(4,128)}), f32[8,4,128]{2,1,0:T(4,128)S(1)}, u32[]{:S(2)}, u32[]{:S(2)}) async-start(f32[8,4,128]{2,1,0:T(4,128)} %bitcast.5), calls=%async_computation | async-start | bytes 32768 | tf_op jit(solution)/shard_map/all_to_all | solution.py:367
  8.8 4.3 %pre.1 = (bf16[512,1024]{1,0:T(8,128)(2,1)}, bf16[512,256]{1,0:T(8,128)(2,1)S(1)}, bf16[512,256]{1,0:T(8,128)(2,1)S(1)}, bf16[512,256]{1,0:T(8,128)(2,1)S(1)}, b...) custom-call(bf16[512,1024]{1,0:T(8,128)(2,1)} %cf.1, bf16[64,1024]{1,0:T(8,128)(2,1)} %pf.1, s32[1,512]{1,0:T(1,128)} %bitcast.6, ...), custom_call_target="tpu_custom_call" | custom-call | tf_op jit(solution)/shard_map/pre/pallas_call | solution.py:404
  13.1 0.0 copy-start.4
  13.1 2.3 %all-to-all-done.gates = f32[8,4,128]{2,1,0:T(4,128)S(1)} async-done(((f32[8,4,128]{2,1,0:T(4,128)}), f32[8,4,128]{2,1,0:T(4,128)S(1)}, u32[]{:S(2)}, u32[]{:S(2)}) %all-to-all-start) | async-done | bytes 16416 | tf_op jit(solution)/shard_map/all_to_all | solution.py:367
  15.4 2.2 %state.1 = (f32[512,256]{1,0:T(8,128)S(1)}, f32[8,512]{1,0:T(8,128)S(1)}, bf16[272,256]{1,0:T(8,128)(2,1)S(1)}, f32[4,64,256]{2,1,0:T(8,128)S(1)}, f32[8,256]{1,...) custom-call(bf16[512,1024]{1,0:T(8,128)(2,1)S(1)} %get-tuple-element.52.taken, ...), custom_call_target="tpu_custom_call" | custom-call | tf_op jit(solution)/shard_map/state/pallas_call | solution.py:445
  17.5 0.6 collective-permute-start.3
  18.1 1.5 %collective-permute-start = (bf16[272,256]{1,0:T(8,128)(2,1)S(1)}, bf16[272,256]{1,0:T(8,128)(2,1)S(1)}, u32[]{:S(2)}, u32[]{:S(2)}) collective-permute-start(bf16[272,256]{1,0:T(8,128)(2,1)S(1)} %get-tuple-element.56), channel_id=1, source_target_pairs={{0,4},{4,0},{8,12},{12,8},{16,20},{20,16},{24,28},{28,24},{1,5},{5... | collective-permute-start | bytes 417800 | tf_op jit(solution)/shard_map/ppermute | solution.py:340
  19.6 0.0 collective-permute-start.10
  19.6 3.2 %collective-permute-done.3.refs_0_ = bf16[272,256]{1,0:T(8,128)(2,1)S(1)} collective-permute-done((bf16[272,256]{1,0:T(8,128)(2,1)S(1)}, bf16[272,256]{1,0:T(8,128)(2,1)S(1)}, u32[]{:S(2)}, u32[]{:S(2)}) %collective-permute-start.3) | collective-permute-done | bytes 139296 | tf_op jit(solution)/shard_map/ppermute | solution.py:340
  22.8 0.1 shard_map.138
  22.9 0.7 %collective-permute-start.4 = (bf16[272,256]{1,0:T(8,128)(2,1)S(1)}, bf16[272,256]{1,0:T(8,128)(2,1)S(1)}, u32[]{:S(2)}, u32[]{:S(2)}) collective-permute-start(bf16[272,256]{1,0:T(8,128)(2,1)S(1)} %get-tuple-element.72), channel_id=1, source_target_pairs={{0,8},{4,12},{8,0},{12,4},{16,24},{20,28},{24,16},{28,20},{1,9},{5... | collective-permute-start | bytes 417800 | tf_op jit(solution)/shard_map/ppermute | solution.py:340
  23.6 0.7 %collective-permute-done.refs_0_ = bf16[272,256]{1,0:T(8,128)(2,1)S(1)} collective-permute-done((bf16[272,256]{1,0:T(8,128)(2,1)S(1)}, bf16[272,256]{1,0:T(8,128)(2,1)S(1)}, u32[]{:S(2)}, u32[]{:S(2)}) %collective-permute-start) | collective-permute-done | bytes 139296 | tf_op jit(solution)/shard_map/ppermute | solution.py:340
  24.3 0.1 shard_map.136
  24.4 0.7 %collective-permute-start.1 = (bf16[272,256]{1,0:T(8,128)(2,1)S(1)}, bf16[272,256]{1,0:T(8,128)(2,1)S(1)}, u32[]{:S(2)}, u32[]{:S(2)}) collective-permute-start(bf16[272,256]{1,0:T(8,128)(2,1)S(1)} %get-tuple-element.59), channel_id=1, source_target_pairs={{0,8},{4,12},{8,0},{12,4},{16,24},{20,28},{24,16},{28,20},{1,9},{5... | collective-permute-start | bytes 417800 | tf_op jit(solution)/shard_map/ppermute | solution.py:340
  25.1 2.9 %collective-permute-done.4.refs_0_ = bf16[272,256]{1,0:T(8,128)(2,1)S(1)} collective-permute-done((bf16[272,256]{1,0:T(8,128)(2,1)S(1)}, bf16[272,256]{1,0:T(8,128)(2,1)S(1)}, u32[]{:S(2)}, u32[]{:S(2)}) %collective-permute-start.4) | collective-permute-done | bytes 139296 | tf_op jit(solution)/shard_map/ppermute | solution.py:340
  28.0 0.1 shard_map.139
  28.1 1.7 %collective-permute-start.5 = (bf16[272,256]{1,0:T(8,128)(2,1)S(1)}, bf16[272,256]{1,0:T(8,128)(2,1)S(1)}, u32[]{:S(2)}, u32[]{:S(2)}) collective-permute-start(bf16[272,256]{1,0:T(8,128)(2,1)S(1)} %get-tuple-element.77), channel_id=1, source_target_pairs={{0,16},{4,20},{8,24},{12,28},{16,0},{20,4},{24,8},{28,12},{1,17},{... | collective-permute-start | bytes 417800 | tf_op jit(solution)/shard_map/ppermute | solution.py:340
  29.8 0.7 collective-permute-done.1.refs_0_
  30.5 0.1 shard_map.137
  30.6 1.3 %collective-permute-start.2 = (bf16[272,256]{1,0:T(8,128)(2,1)S(1)}, bf16[272,256]{1,0:T(8,128)(2,1)S(1)}, u32[]{:S(2)}, u32[]{:S(2)}) collective-permute-start(bf16[272,256]{1,0:T(8,128)(2,1)S(1)} %get-tuple-element.64), channel_id=1, source_target_pairs={{0,16},{4,20},{8,24},{12,28},{16,0},{20,4},{24,8},{28,12},{1,17},{... | collective-permute-start | bytes 417800 | tf_op jit(solution)/shard_map/ppermute | solution.py:340
  31.8 1.7 %inside.1.refs_13_ = f32[512,256]{1,0:T(8,128)S(1)} custom-call(bf16[512,256]{1,0:T(8,128)(2,1)S(1)} %get-tuple-element.82.q.refs_10_, bf16[512,256]{1,0:T(8,128)(2,1)S(1)} %get-tuple-element.53.k, bf16[512,256]{1,0:T(8,128)(2,1)S(1)} %get-tuple-element.54.v, f32[512,256]{1,0:T(8,128)S(1)} %get-tuple-element.83.c_lanes.refs_12_, ...), custom_call_target="tpu_custom_call" | custom-call | tf_op jit(solution)/shard_map/inside/pallas_call | solution.py:455
  33.5 6.1 %collective-permute-done.5.refs_5_ = bf16[272,256]{1,0:T(8,128)(2,1)S(1)} collective-permute-done((bf16[272,256]{1,0:T(8,128)(2,1)S(1)}, bf16[272,256]{1,0:T(8,128)(2,1)S(1)}, u32[]{:S(2)}, u32[]{:S(2)}) %collective-permute-start.5) | collective-permute-done | bytes 139296 | tf_op jit(solution)/shard_map/ppermute | solution.py:340
  39.6 1.6 %collective-permute-done.2.refs_0_ = bf16[272,256]{1,0:T(8,128)(2,1)S(1)} collective-permute-done((bf16[272,256]{1,0:T(8,128)(2,1)S(1)}, bf16[272,256]{1,0:T(8,128)(2,1)S(1)}, u32[]{:S(2)}, u32[]{:S(2)}) %collective-permute-start.2) | collective-permute-done | bytes 139296 | tf_op jit(solution)/shard_map/ppermute | solution.py:340
  41.2 1.7 %outside.1 = (bf16[256,256]{1,0:T(8,128)(2,1)S(1)}, bf16[256,256]{1,0:T(8,128)(2,1)S(1)}) custom-call(bf16[272,256]{1,0:T(8,128)(2,1)S(1)} %collective-permute-done.2.refs_0_, f32[4,64,256]{2,1,0:T(8,128)S(1)} %get-tuple-element.65.refs_1_, f32[8,256]{1,0:T(8,128)S(1)} %get-tuple-element.66.refs_2_, f32[4,64,256]{2,1,0:T(8,128)S(1)} %get-tuple-element.67.refs_3_, ...), custom_call_target="tpu_custom_call" | custom-call | tf_op jit(solution)/shard_map/outside/pallas_call | solution.py:479
  42.9 0.6 collective-permute-start.15
  43.5 0.0 collective-permute-start.8
  43.5 0.5 collective-permute-start.9
  44.0 3.9 %collective-permute-done.15.refs_0_ = bf16[256,256]{1,0:T(8,128)(2,1)S(1)} collective-permute-done((bf16[256,256]{1,0:T(8,128)(2,1)S(1)}, bf16[256,256]{1,0:T(8,128)(2,1)S(1)}, u32[]{:S(2)}, u32[]{:S(2)}) %collective-permute-start.15) | collective-permute-done | bytes 131104 | tf_op jit(solution)/shard_map/ppermute | solution.py:340
  47.9 0.6 collective-permute-start.6
  48.5 0.0 collective-permute-done.8.refs_2_
  48.5 0.0 collective-permute-done.9.refs_3_
  48.5 0.0 collective-permute-done.12.refs_7_
  48.6 0.2 copy-done.2
  48.7 0.6 copy-done.3
  49.4 3.3 %load.1 = (f32[512,1024]{1,0:T(8,128)S(1)}, bf16[2,256,1024]{2,1,0:T(8,128)(2,1)S(1)}, f32[1,1024]{1,0:T(1,128)S(1)}, bf16[1024,1024]{1,0:T(8,128)(2,1)S(1)}, bf16[1024,1024]{1,0:T(8,128)(2,1)S(1)}) custom-call(bf16[256,256]{1,0:T(8,128)(2,1)S(1)} %get-tuple-element.85.refs_0_, bf16[256,256]{1,0:T(8,128)(2,1)S(1)} %get-tuple-element.86.refs_1_, ...), custom_call_target="tpu_custom_call" | custom-call | tf_op jit(solution)/shard_map/load/pallas_call | solution.py:514
  52.6 1.9 %shard_map.141 = (f32[256,256]{1,0:T(8,128)S(1)}, f32[256,256]{1,0:T(8,128)S(1)}, bf16[256,512]{1,0:T(8,128)(2,1)S(1)}) custom-call(bf16[256,256]{1,0:T(8,128)(2,1)S(1)} %collective-permute-done.15.refs_0_, bf16[256,256]{1,0:T(8,128)(2,1)S(1)} %collective-permute-done.16.refs_1_, f32[512,1024]{1,0:T(8,128)S(1)} %get-tuple-element.88.refs_2_, ...), custom_call_target="tpu_custom_call" | custom-call | tf_op jit(solution)/shard_map/pallas_call | solution.py:527
  54.6 0.2 collective-permute-start.17
  54.8 0.0 collective-permute-done.6.refs_0_
  54.8 0.4 collective-permute-start.7
  55.2 1.2 %collective-permute-done.7.refs_1_ = bf16[256,256]{1,0:T(8,128)(2,1)S(1)} collective-permute-done((bf16[256,256]{1,0:T(8,128)(2,1)S(1)}, bf16[256,256]{1,0:T(8,128)(2,1)S(1)}, u32[]{:S(2)}, u32[]{:S(2)}) %collective-permute-start.7) | collective-permute-done | bytes 131104 | tf_op jit(solution)/shard_map/ppermute | solution.py:340
  56.4 1.9 %shard_map.140 = (f32[256,256]{1,0:T(8,128)S(1)}, f32[256,256]{1,0:T(8,128)S(1)}, bf16[256,512]{1,0:T(8,128)(2,1)S(1)}) custom-call(bf16[256,256]{1,0:T(8,128)(2,1)S(1)} %collective-permute-done.6.refs_0_, bf16[256,256]{1,0:T(8,128)(2,1)S(1)} %collective-permute-done.7.refs_1_, f32[512,1024]{1,0:T(8,128)S(1)} %get-tuple-element.88.refs_2_, ...), custom_call_target="tpu_custom_call" | custom-call | tf_op jit(solution)/shard_map/pallas_call | solution.py:527
  58.3 0.2 collective-permute-start.13
  58.5 1.6 %collective-permute-start.18 = (bf16[256,256]{1,0:T(8,128)(2,1)S(1)}, bf16[256,256]{1,0:T(8,128)(2,1)S(1)}, u32[]{:S(2)}, u32[]{:S(2)}) collective-permute-start(bf16[256,256]{1,0:T(8,128)(2,1)S(1)} %add_convert_fusion), channel_id=1, source_target_pairs={{0,2},{1,3},{2,0},{3,1},{4,6},{5,7},{6,4},{7,5},{8,10},{9,11},{10,... | collective-permute-start | bytes 393224 | tf_op jit(solution)/shard_map/ppermute | solution.py:340
  60.2 1.3 %collective-permute-start.14 = (bf16[256,256]{1,0:T(8,128)(2,1)S(1)}, bf16[256,256]{1,0:T(8,128)(2,1)S(1)}, u32[]{:S(2)}, u32[]{:S(2)}) collective-permute-start(bf16[256,256]{1,0:T(8,128)(2,1)S(1)} %add_convert_fusion.1), channel_id=1, source_target_pairs={{0,2},{1,3},{2,0},{3,1},{4,6},{5,7},{6,4},{7,5},{8,10},{9,11},{10,... | collective-permute-start | bytes 393224 | tf_op jit(solution)/shard_map/ppermute | solution.py:340
  61.5 3.5 %collective-permute-done.18.refs_5_ = bf16[256,256]{1,0:T(8,128)(2,1)S(1)} collective-permute-done((bf16[256,256]{1,0:T(8,128)(2,1)S(1)}, bf16[256,256]{1,0:T(8,128)(2,1)S(1)}, u32[]{:S(2)}, u32[]{:S(2)}) %collective-permute-start.18) | collective-permute-done | bytes 131104 | tf_op jit(solution)/shard_map/ppermute | solution.py:340
  65.0 2.2 %collective-permute-done.14.refs_2_ = bf16[256,256]{1,0:T(8,128)(2,1)S(1)} collective-permute-done((bf16[256,256]{1,0:T(8,128)(2,1)S(1)}, bf16[256,256]{1,0:T(8,128)(2,1)S(1)}, u32[]{:S(2)}, u32[]{:S(2)}) %collective-permute-start.14) | collective-permute-done | bytes 131104 | tf_op jit(solution)/shard_map/ppermute | solution.py:340
  67.2 0.8 %final.1 = bf16[512,256]{1,0:T(8,128)(2,1)} custom-call(f32[256,256]{1,0:T(8,128)S(1)} %get-tuple-element.93.refs_0_, bf16[256,512]{1,0:T(8,128)(2,1)S(1)} %collective-permute-done.13.refs_1_, bf16[256,256]{1,0:T(8,128)(2,1)S(1)} %collective-permute-done.14.refs_2_, f32[256,256]{1,0:T(8,128)S(1)} %get-tuple-element.96.refs_3_, ...), custom_call_target="tpu_custom_call" | custom-call | tf_op jit(solution)/shard_map/final/pallas_call | solution.py:550
  (17 shorter events, 0.1 us)
Async XLA Ops:
  0.0 25.1 %collective-permute-start.11 = (bf16[256,1024]{1,0:T(8,128)(2,1)}, bf16[256,1024]{1,0:T(8,128)(2,1)S(1)}, u32[]{:S(2)}, u32[]{:S(2)}) collective-permute-start(bf16[256,1024]{1,0:T(8,128)(2,1)} %refs_4_.1), channel_id=1, source_target_pairs={{0,2},{1,3},{2,0},{3,1},{4,6},{5,7},{6,4},{7,5},{8,10},{9,11},{10,... | collective-permute-start | bytes 1572872 | tf_op jit(solution)/shard_map/ppermute | solution.py:340
  3.0 12.4 %all-to-all-start = ((f32[8,4,128]{2,1,0:T(4,128)}), f32[8,4,128]{2,1,0:T(4,128)S(1)}, u32[]{:S(2)}, u32[]{:S(2)}) async-start(f32[8,4,128]{2,1,0:T(4,128)} %bitcast.5), calls=%async_computation | async-start | bytes 32768 | tf_op jit(solution)/shard_map/all_to_all | solution.py:367
  8.8 10.8 %copy-start = (bf16[256,1024]{1,0:T(8,128)(2,1)S(1)}, bf16[256,1024]{1,0:T(8,128)(2,1)}, u32[]{:S(2)}) copy-start(bf16[256,1024]{1,0:T(8,128)(2,1)} %refs_4_.1) | copy-start | bytes 1572868
  13.1 18.7 %copy-start.4 = (bf16[256]{0:T(256)(128)(2,1)S(1)}, bf16[256]{0:T(256)(128)(2,1)}, u32[]{:S(2)}) copy-start(bf16[256]{0:T(256)(128)(2,1)} %param.23) | copy-start | bytes 1540
  17.5 5.3 %collective-permute-start.3 = (bf16[272,256]{1,0:T(8,128)(2,1)S(1)}, bf16[272,256]{1,0:T(8,128)(2,1)S(1)}, u32[]{:S(2)}, u32[]{:S(2)}) collective-permute-start(bf16[272,256]{1,0:T(8,128)(2,1)S(1)} %get-tuple-element.69), channel_id=1, source_target_pairs={{0,4},{4,0},{8,12},{12,8},{16,20},{20,16},{24,28},{28,24},{1,5},{5... | collective-permute-start | bytes 417800 | tf_op jit(solution)/shard_map/ppermute | solution.py:340
  18.1 6.2 %collective-permute-start = (bf16[272,256]{1,0:T(8,128)(2,1)S(1)}, bf16[272,256]{1,0:T(8,128)(2,1)S(1)}, u32[]{:S(2)}, u32[]{:S(2)}) collective-permute-start(bf16[272,256]{1,0:T(8,128)(2,1)S(1)} %get-tuple-element.56), channel_id=1, source_target_pairs={{0,4},{4,0},{8,12},{12,8},{16,20},{20,16},{24,28},{28,24},{1,5},{5... | collective-permute-start | bytes 417800 | tf_op jit(solution)/shard_map/ppermute | solution.py:340
  19.6 28.3 %collective-permute-start.10 = (bf16[256,1024]{1,0:T(8,128)(2,1)S(1)}, bf16[256,1024]{1,0:T(8,128)(2,1)S(1)}, u32[]{:S(2)}, u32[]{:S(2)}) collective-permute-start(bf16[256,1024]{1,0:T(8,128)(2,1)S(1)} %copy-done), channel_id=1, source_target_pairs={{0,1},{1,0},{2,3},{3,2},{4,5},{5,4},{6,7},{7,6},{8,9},{9,8},{10,11... | collective-permute-start | bytes 1572872 | tf_op jit(solution)/shard_map/ppermute | solution.py:340
  22.9 5.1 %collective-permute-start.4 = (bf16[272,256]{1,0:T(8,128)(2,1)S(1)}, bf16[272,256]{1,0:T(8,128)(2,1)S(1)}, u32[]{:S(2)}, u32[]{:S(2)}) collective-permute-start(bf16[272,256]{1,0:T(8,128)(2,1)S(1)} %get-tuple-element.72), channel_id=1, source_target_pairs={{0,8},{4,12},{8,0},{12,4},{16,24},{20,28},{24,16},{28,20},{1,9},{5... | collective-permute-start | bytes 417800 | tf_op jit(solution)/shard_map/ppermute | solution.py:340
  24.4 6.1 %collective-permute-start.1 = (bf16[272,256]{1,0:T(8,128)(2,1)S(1)}, bf16[272,256]{1,0:T(8,128)(2,1)S(1)}, u32[]{:S(2)}, u32[]{:S(2)}) collective-permute-start(bf16[272,256]{1,0:T(8,128)(2,1)S(1)} %get-tuple-element.59), channel_id=1, source_target_pairs={{0,8},{4,12},{8,0},{12,4},{16,24},{20,28},{24,16},{28,20},{1,9},{5... | collective-permute-start | bytes 417800 | tf_op jit(solution)/shard_map/ppermute | solution.py:340
  25.1 17.8 %copy-start.1 = (bf16[256,1024]{1,0:T(8,128)(2,1)}, bf16[256,1024]{1,0:T(8,128)(2,1)S(1)}, u32[]{:S(2)}) copy-start(bf16[256,1024]{1,0:T(8,128)(2,1)S(1)} %collective-permute-done.11.refs_6_) | copy-start | bytes 1572868
  25.1 23.4 %collective-permute-start.12 = (bf16[256,1024]{1,0:T(8,128)(2,1)S(1)}, bf16[256,1024]{1,0:T(8,128)(2,1)S(1)}, u32[]{:S(2)}, u32[]{:S(2)}) collective-permute-start(bf16[256,1024]{1,0:T(8,128)(2,1)S(1)} %collective-permute-done.11.refs_6_), channel_id=1, source_target_pairs={{0,1},{1,0},{2,3},{3,2},{4,5},{5,4},{6,7},{7,6},{8,9},{9,8},{10,11... | collective-permute-start | bytes 1572872 | tf_op jit(solution)/shard_map/ppermute | solution.py:340
  28.1 11.6 %collective-permute-start.5 = (bf16[272,256]{1,0:T(8,128)(2,1)S(1)}, bf16[272,256]{1,0:T(8,128)(2,1)S(1)}, u32[]{:S(2)}, u32[]{:S(2)}) collective-permute-start(bf16[272,256]{1,0:T(8,128)(2,1)S(1)} %get-tuple-element.77), channel_id=1, source_target_pairs={{0,16},{4,20},{8,24},{12,28},{16,0},{20,4},{24,8},{28,12},{1,17},{... | collective-permute-start | bytes 417800 | tf_op jit(solution)/shard_map/ppermute | solution.py:340
  30.6 10.6 %collective-permute-start.2 = (bf16[272,256]{1,0:T(8,128)(2,1)S(1)}, bf16[272,256]{1,0:T(8,128)(2,1)S(1)}, u32[]{:S(2)}, u32[]{:S(2)}) collective-permute-start(bf16[272,256]{1,0:T(8,128)(2,1)S(1)} %get-tuple-element.64), channel_id=1, source_target_pairs={{0,16},{4,20},{8,24},{12,28},{16,0},{20,4},{24,8},{28,12},{1,17},{... | collective-permute-start | bytes 417800 | tf_op jit(solution)/shard_map/ppermute | solution.py:340
  42.9 5.0 %collective-permute-start.15 = (bf16[256,256]{1,0:T(8,128)(2,1)S(1)}, bf16[256,256]{1,0:T(8,128)(2,1)S(1)}, u32[]{:S(2)}, u32[]{:S(2)}) collective-permute-start(bf16[256,256]{1,0:T(8,128)(2,1)S(1)} %get-tuple-element.86.refs_1_), channel_id=1, source_target_pairs={{0,2},{1,3},{2,0},{3,1},{4,6},{5,7},{6,4},{7,5},{8,10},{9,11},{10,... | collective-permute-start | bytes 393224 | tf_op jit(solution)/shard_map/ppermute | solution.py:340
  43.5 5.0 %collective-permute-start.8 = (bf16[256,256]{1,0:T(8,128)(2,1)S(1)}, bf16[256,256]{1,0:T(8,128)(2,1)S(1)}, u32[]{:S(2)}, u32[]{:S(2)}) collective-permute-start(bf16[256,256]{1,0:T(8,128)(2,1)S(1)} %get-tuple-element.85.refs_0_), channel_id=1, source_target_pairs={{0,1},{1,0},{2,3},{3,2},{4,5},{5,4},{6,7},{7,6},{8,9},{9,8},{10,11... | collective-permute-start | bytes 393224 | tf_op jit(solution)/shard_map/ppermute | solution.py:340
  43.5 5.0 %collective-permute-start.9 = (bf16[256,256]{1,0:T(8,128)(2,1)S(1)}, bf16[256,256]{1,0:T(8,128)(2,1)S(1)}, u32[]{:S(2)}, u32[]{:S(2)}) collective-permute-start(bf16[256,256]{1,0:T(8,128)(2,1)S(1)} %get-tuple-element.86.refs_1_), channel_id=1, source_target_pairs={{0,1},{1,0},{2,3},{3,2},{4,5},{5,4},{6,7},{7,6},{8,9},{9,8},{10,11... | collective-permute-start | bytes 393224 | tf_op jit(solution)/shard_map/ppermute | solution.py:340
  47.9 4.7 %collective-permute-start.16 = (bf16[256,256]{1,0:T(8,128)(2,1)S(1)}, bf16[256,256]{1,0:T(8,128)(2,1)S(1)}, u32[]{:S(2)}, u32[]{:S(2)}) collective-permute-start(bf16[256,256]{1,0:T(8,128)(2,1)S(1)} %collective-permute-done.15.refs_0_), channel_id=1, source_target_pairs={{0,1},{1,0},{2,3},{3,2},{4,5},{5,4},{6,7},{7,6},{8,9},{9,8},{10,11... | collective-permute-start | bytes 393224 | tf_op jit(solution)/shard_map/ppermute | solution.py:340
  47.9 0.8 %copy-start.2 = (bf16[256,1024]{1,0:T(8,128)(2,1)}, bf16[256,1024]{1,0:T(8,128)(2,1)S(1)}, u32[]{:S(2)}) copy-start(bf16[256,1024]{1,0:T(8,128)(2,1)S(1)} %collective-permute-done.10.refs_5_) | copy-start | bytes 1572868
  47.9 6.9 %collective-permute-start.6 = (bf16[256,256]{1,0:T(8,128)(2,1)S(1)}, bf16[256,256]{1,0:T(8,128)(2,1)S(1)}, u32[]{:S(2)}, u32[]{:S(2)}) collective-permute-start(bf16[256,256]{1,0:T(8,128)(2,1)S(1)} %get-tuple-element.85.refs_0_), channel_id=1, source_target_pairs={{0,2},{1,3},{2,0},{3,1},{4,6},{5,7},{6,4},{7,5},{8,10},{9,11},{10,... | collective-permute-start | bytes 393224 | tf_op jit(solution)/shard_map/ppermute | solution.py:340
  48.5 0.8 %copy-start.3 = (bf16[256,1024]{1,0:T(8,128)(2,1)}, bf16[256,1024]{1,0:T(8,128)(2,1)S(1)}, u32[]{:S(2)}) copy-start(bf16[256,1024]{1,0:T(8,128)(2,1)S(1)} %collective-permute-done.12.refs_7_) | copy-start | bytes 1572868
  54.6 3.9 %collective-permute-start.17 = (bf16[256,512]{1,0:T(8,128)(2,1)S(1)}, bf16[256,512]{1,0:T(8,128)(2,1)S(1)}, u32[]{:S(2)}, u32[]{:S(2)}) collective-permute-start(bf16[256,512]{1,0:T(8,128)(2,1)S(1)} %get-tuple-element.97), channel_id=1, source_target_pairs={{0,1},{1,0},{2,3},{3,2},{4,5},{5,4},{6,7},{7,6},{8,9},{9,8},{10,11... | collective-permute-start | bytes 786440 | tf_op jit(solution)/shard_map/ppermute | solution.py:340
  54.8 1.6 %collective-permute-start.7 = (bf16[256,256]{1,0:T(8,128)(2,1)S(1)}, bf16[256,256]{1,0:T(8,128)(2,1)S(1)}, u32[]{:S(2)}, u32[]{:S(2)}) collective-permute-start(bf16[256,256]{1,0:T(8,128)(2,1)S(1)} %collective-permute-done.6.refs_0_), channel_id=1, source_target_pairs={{0,1},{1,0},{2,3},{3,2},{4,5},{5,4},{6,7},{7,6},{8,9},{9,8},{10,11... | collective-permute-start | bytes 393224 | tf_op jit(solution)/shard_map/ppermute | solution.py:340
  58.3 1.8 %collective-permute-start.13 = (bf16[256,512]{1,0:T(8,128)(2,1)S(1)}, bf16[256,512]{1,0:T(8,128)(2,1)S(1)}, u32[]{:S(2)}, u32[]{:S(2)}) collective-permute-start(bf16[256,512]{1,0:T(8,128)(2,1)S(1)} %get-tuple-element.94), channel_id=1, source_target_pairs={{0,1},{1,0},{2,3},{3,2},{4,5},{5,4},{6,7},{7,6},{8,9},{9,8},{10,11... | collective-permute-start | bytes 786440 | tf_op jit(solution)/shard_map/ppermute | solution.py:340
  58.5 6.4 %collective-permute-start.18 = (bf16[256,256]{1,0:T(8,128)(2,1)S(1)}, bf16[256,256]{1,0:T(8,128)(2,1)S(1)}, u32[]{:S(2)}, u32[]{:S(2)}) collective-permute-start(bf16[256,256]{1,0:T(8,128)(2,1)S(1)} %add_convert_fusion), channel_id=1, source_target_pairs={{0,2},{1,3},{2,0},{3,1},{4,6},{5,7},{6,4},{7,5},{8,10},{9,11},{10,... | collective-permute-start | bytes 393224 | tf_op jit(solution)/shard_map/ppermute | solution.py:340
  60.2 7.0 %collective-permute-start.14 = (bf16[256,256]{1,0:T(8,128)(2,1)S(1)}, bf16[256,256]{1,0:T(8,128)(2,1)S(1)}, u32[]{:S(2)}, u32[]{:S(2)}) collective-permute-start(bf16[256,256]{1,0:T(8,128)(2,1)S(1)} %add_convert_fusion.1), channel_id=1, source_target_pairs={{0,2},{1,3},{2,0},{3,1},{4,6},{5,7},{6,4},{7,5},{8,10},{9,11},{10,... | collective-permute-start | bytes 393224 | tf_op jit(solution)/shard_map/ppermute | solution.py:340
